TPU v7x, 256 devices: a whole 4x4x8 slice. The times are simulated.
256 devices in a mesh: scene: 4 (over y), space: 64 (over z, x, core).
Axes of the slice: x: 4, y: 4, z: 8, core: 2. Of those that a mesh axis runs over, the one named last changes fastest.
Arguments:
- features: bfloat16 [4, 49152, 128], P('scene', 'space'), may hold values from -6 to 6
- cotangent: bfloat16 [4, 49152, 128], P('scene', 'space'), may hold values from -0.09375 to 0.09375
- conv_weight: bfloat16 [3456, 128], replicated, may hold values from -0.109375 to 0.109375
- down_weight: bfloat16 [1024, 256], replicated, may hold values from -0.1875 to 0.1875
- up_weight: bfloat16 [256, 1024], replicated, may hold values from -0.375 to 0.375
- live_count: int32 [4, 64], P('scene', 'space'), may hold values from 256 to 768, as said below
- neighbours: int32 [4, 26, 49152], P('scene', None, 'space'), may hold values from -1 to 959, as said below
- destination: int32 [4, 49152, 1], P('scene', 'space'), may hold values from 0 to 63; in each aligned block of 768 rows (0 to 767, 768 to 1535, ..., all dimensions but the last counted through in order) at most 24 rows name the same one
- assemble: int32 [4, 64, 1536], P('scene', 'space'), may hold values from 0 to 1535, each once within a row
Outputs:
- output: bfloat16 [4, 49152, 128], P('scene', 'space')
- grad_conv: float32 [3456, 128], replicated
- grad_down: float32 [1024, 256], replicated
- grad_up: float32 [256, 1024], replicated
Inputs may be any that keep to these rules, and one draw needn't show every extreme that they name: The live slots of a device are its first live_count slots; on each scene some device has all 768 slots live. Only live slots have neighbours, all live and other than the slot itself. A code of 768 or more occurs only for slots below 96 (codes below 864, device s - 1 exists) or slots from 96 to 2 * 96 - 1 (codes from 864, device s + 1 exists). `destination`: among the rows of one device no owner is named more than 24 times, a bound that some block reaches. `assemble`: A permutation of the received rows of each device.
All inputs are finite; a program needn't handle non-finite values.
Results may differ from a plain program's by a relative error of at most 0.0053.
Values may be sent and summed in bfloat16 or wider, within the bound.
A program may use at most 64 MiB of HBM per device.

v0:
```python
import jax
import jax.numpy as jnp
from jax import lax
from jax.sharding import PartitionSpec as P


def extended(block, sides, width):
    for axis, dim in sides:
        count = lax.axis_size(axis)
        forward = [(i, i + 1) for i in range(count - 1)]
        backward = [(target, source) for source, target in forward]
        low = lax.ppermute(
            lax.slice_in_dim(block, block.shape[dim] - width, None, axis=dim), axis, forward
        )
        high = lax.ppermute(lax.slice_in_dim(block, 0, width, axis=dim), axis, backward)
        block = jnp.concatenate([low, block, high], axis=dim)
    return block


def silu_grad(value):
    sigma = jax.nn.sigmoid(value)
    return sigma * (1.0 + value * (1.0 - sigma))


def contract_rows(left, right):
    return lax.dot_general(
        left, right, (((0,), (0,)), ((), ())), preferred_element_type=jnp.float32
    )


def contract_cols(left, right):
    return lax.dot_general(
        left, right, (((1,), (1,)), ((), ())), preferred_element_type=jnp.float32
    )


def on_device(
    features,
    cotangent,
    conv_weight,
    down_weight,
    up_weight,
    live_count,
    neighbours,
    destination,
    assemble,
):
    slots = features.shape[1]
    width = features.shape[2]
    places = lax.axis_size("space")
    rim = slots // 8
    cap = 2 * slots // places
    zero_b = jnp.zeros((), jnp.bfloat16)
    live = (jnp.arange(slots, dtype=jnp.int32) < live_count[0, 0])[:, None]
    own = jnp.where(live, features[0], zero_b)
    grad_rows = jnp.where(live, cotangent[0], zero_b)
    dest = destination[0, :, 0]
    onehot = (dest[:, None] == jnp.arange(places, dtype=jnp.int32)[None, :]).astype(jnp.int32)
    rank = jnp.sum((jnp.cumsum(onehot, axis=0) - onehot) * onehot, axis=1)
    target = dest * cap + rank

    def pack(rows):
        return (
            jnp.zeros((2 * slots, width), rows.dtype)
            .at[target]
            .set(rows)
            .reshape(places, cap, width)
        )

    codes = neighbours[0].T
    zero_row = jnp.zeros((1, width), jnp.bfloat16)
    padded = extended(own[None], (("space", 0),), 1)
    table = jnp.concatenate([padded.reshape(3 * slots, width), zero_row], axis=0)
    index = jnp.where(
        codes < slots,
        slots + codes,
        jnp.where(codes < slots + rim, rim + codes - slots, 2 * slots + codes - slots - rim),
    )
    index = jnp.where(codes < 0, 3 * slots, index)
    rows = table[index]
    stacked = jnp.concatenate([own[:, None, :], rows], axis=1).reshape(slots, 27 * width)
    pre_conv = jnp.dot(stacked, conv_weight, preferred_element_type=jnp.float32)
    mixed = jnp.where(live, own.astype(jnp.float32) + jax.nn.silu(pre_conv), 0.0).astype(
        jnp.bfloat16
    )
    stacked, pre_conv, mixed = (stacked, pre_conv, mixed)
    got_mixed, got_grad = (
        lax.all_to_all(pack(mixed), "space", split_axis=0, concat_axis=0, tiled=True),
        lax.all_to_all(pack(grad_rows), "space", split_axis=0, concat_axis=0, tiled=True),
    )
    order = assemble[0, 0]
    coarse_rows = 2 * slots // 8
    coarse_in = got_mixed.reshape(2 * slots, width)[order].reshape(coarse_rows, 8 * width)
    coarse_grad = got_grad.reshape(2 * slots, width)[order].reshape(coarse_rows, 8 * width)
    pre = jnp.dot(coarse_in, down_weight, preferred_element_type=jnp.float32)
    coarse = jax.nn.silu(pre).astype(jnp.bfloat16)
    up_rows = jnp.dot(coarse, up_weight, preferred_element_type=jnp.float32).astype(jnp.bfloat16)
    grad_up = contract_rows(coarse, coarse_grad)
    back = contract_cols(coarse_grad, up_weight)
    grad_pre = (back * silu_grad(pre)).astype(jnp.bfloat16)
    grad_down = contract_rows(coarse_in, grad_pre)
    grad_in = contract_cols(grad_pre, down_weight).astype(jnp.bfloat16)

    def unpack(rows):
        return (
            jnp.zeros((2 * slots, width), jnp.bfloat16)
            .at[order]
            .set(rows.reshape(2 * slots, width))
            .reshape(places, cap, width)
        )

    got_up, got_back = (
        lax.all_to_all(unpack(up_rows), "space", split_axis=0, concat_axis=0, tiled=True),
        lax.all_to_all(unpack(grad_in), "space", split_axis=0, concat_axis=0, tiled=True),
    )
    fine_up = got_up.reshape(2 * slots, width)[target]
    fine_back = got_back.reshape(2 * slots, width)[target]
    output = jnp.where(live, mixed.astype(jnp.float32) + fine_up.astype(jnp.float32), 0.0).astype(
        jnp.bfloat16
    )
    grad_mixed = jnp.where(live, grad_rows.astype(jnp.float32) + fine_back.astype(jnp.float32), 0.0)
    grad_conv_pre = (grad_mixed * silu_grad(pre_conv)).astype(jnp.bfloat16)
    grad_conv = contract_rows(stacked, grad_conv_pre)
    grad_conv, grad_down, grad_up = lax.psum((grad_conv, grad_down, grad_up), ("scene", "space"))
    return (output[None], grad_conv, grad_down, grad_up)


def solution(mesh):
    in_specs = (
        P("scene", "space", None),
        P("scene", "space", None),
        P(),
        P(),
        P(),
        P("scene", "space"),
        P("scene", None, "space"),
        P("scene", "space", None),
        P("scene", "space", None),
    )
    out_specs = (P("scene", "space", None), P(), P(), P())
    return jax.shard_map(
        on_device, mesh=mesh, in_specs=in_specs, out_specs=out_specs, check_vma=False
    )
```

profile of v0, /device:TPU:1, one launch (start us, length us, event | category | flops | bytes accessed | tf_op | source)
XLA Modules:
  0.0 463.5 jit_solution(17209846092674494932)
XLA Ops:
  7.9 1.1 broadcast_select_fusion
  9.0 4.5 collective-permute-start
  13.5 1.9 collective-permute-start.1
  15.5 0.7 reduce.1
  16.2 1.8 reduce-window.6
  18.0 0.3 slice_reduce_fusion
  18.3 0.1 fusion.5
  18.4 0.7 fusion.19
  19.1 6.0 %scatter_custom_fusion.2 = bf16[1536,128]{1,0:T(8,128)(2,1)} fusion(s32[768]{0:T(1024)S(1)} %fusion.19, bf16[]{:T(256)} %constant.12.clone.1, bf16[1,768,128]{2,1,0:T(8,128)(2,1)} %param.10, pred[768]{0:T(1024)(128)(4,1)S(1)} %iota_compare_fusion.2), kind=kCustom, calls=%fused_computation.40 | custom fusion | flops 98304 | bytes 591872 | tf_op jit(solution)/shard_map/scatter | solution.py:66
  25.1 13.0 %all-to-all-start.2 = ((bf16[64,24,128]{2,1,0:T(8,128)(2,1)}), bf16[64,24,128]{2,1,0:T(8,128)(2,1)S(1)}, u32[]{:S(2)}, u32[]{:S(2)}) async-start(bf16[64,24,128]{2,1,0:T(8,128)(2,1)} %bitcast.15), calls=%async_computation.2 | async-start | bytes 786432 | tf_op jit(solution)/shard_map/all_to_all | solution.py:89
  38.1 1.1 bitcast_select_fusion.1
  39.2 1.1 compare_select_fusion.2
  40.3 0.2 copy.17
  40.5 0.3 reshape.195
  40.8 0.3 copy.18
  41.3 40.5 %gather_fusion = bf16[19968,128]{1,0:T(8,128)(2,1)} fusion(bf16[2305,128]{1,0:T(8,128)(2,1)S(1)} %concatenate.10, s32[20480]{0:T(1024)S(1)} %pad_clamp_fusion), kind=kCustom, calls=%fused_computation | custom fusion | bytes 10303488 | tf_op jit(solution)/shard_map/gather | solution.py:80
  81.8 9.1 %reshape.194 = bf16[768,26,128]{2,1,0:T(8,128)(2,1)} reshape(bf16[19968,128]{1,0:T(8,128)(2,1)} %gather_fusion) | data formatting | bytes 10223616 | tf_op jit(solution)/shard_map/gather | solution.py:80
  90.8 8.9 %pad_maximum_fusion = bf16[768,27,128]{2,1,0:T(8,128)(2,1)} fusion(bf16[768,26,128]{2,1,0:T(8,128)(2,1)} %reshape.194, bf16[768,1,128]{2,1,0:T(2,128)(2,1)S(1)} %copy.18), kind=kLoop, calls=%fused_computation.9 | loop fusion | flops 10616832 | bytes 10616832 | tf_op jit(solution)/shard_map/concatenate | solution.py:81
  99.7 9.0 %copy.19 = bf16[768,27,128]{0,2,1:T(8,128)(2,1)} copy(bf16[768,27,128]{2,1,0:T(8,128)(2,1)} %pad_maximum_fusion) | data formatting | bytes 10616832 | tf_op jit(solution)/shard_map/concatenate | solution.py:81
  108.7 4.9 %select_convert_fusion.1 = (bf16[768,128]{1,0:T(8,128)(2,1)S(1)}, f32[768,128]{1,0:T(8,128)}) fusion(bf16[1,768,128]{2,1,0:T(8,128)(2,1)S(1)} %copy-done.3, pred[768]{0:T(1024)(128)(4,1)S(1)} %iota_compare_fusion.2, bf16[768,3456]{0,1:T(8,128)(2,1)} %bitcast.74, bf16[3456,128]{1,0:T(8,128)(2,1)S(1)} %copy-done), kind=kOutput, calls=%fused_computation.17 | convolution fusion | flops 680361984 | bytes 6980352 | tf_op jit(solution)/shard_map/dot_general | solution.py:82
  113.6 5.0 %scatter_custom_fusion = bf16[1536,128]{1,0:T(8,128)(2,1)} fusion(s32[768]{0:T(1024)S(1)} %fusion.19, bf16[768,128]{1,0:T(8,128)(2,1)S(1)} %get-tuple-element.7, bf16[]{:T(256)} %constant.12.clone.1), kind=kCustom, calls=%fused_computation.44 | custom fusion | bytes 393218 | tf_op jit(solution)/shard_map/scatter | solution.py:66
  118.6 10.3 %all-to-all-start = ((bf16[64,24,128]{2,1,0:T(8,128)(2,1)}), bf16[64,24,128]{2,1,0:T(8,128)(2,1)S(1)}, u32[]{:S(2)}, u32[]{:S(2)}) async-start(bf16[64,24,128]{2,1,0:T(8,128)(2,1)} %bitcast.9), calls=%async_computation | async-start | bytes 786432 | tf_op jit(solution)/shard_map/all_to_all | solution.py:88
  129.0 3.2 gather_fusion.3
  132.2 0.2 reshape.187
  132.3 11.7 %all-to-all-done = bf16[64,24,128]{2,1,0:T(8,128)(2,1)S(1)} async-done(((bf16[64,24,128]{2,1,0:T(8,128)(2,1)}), bf16[64,24,128]{2,1,0:T(8,128)(2,1)S(1)}, u32[]{:S(2)}, u32[]{:S(2)}) %all-to-all-start) | async-done | bytes 393248 | tf_op jit(solution)/shard_map/all_to_all | solution.py:88
  144.1 3.2 gather_fusion.1
  147.3 0.2 reshape.181
  147.5 0.3 fusion.24
  147.7 1.4 fusion
  149.1 0.3 convolution_convert_fusion
  149.4 0.2 reshape.261
  149.6 5.2 %scatter_custom_fusion.3 = bf16[1536,128]{1,0:T(8,128)(2,1)} fusion(s32[1536]{0:T(1024)S(1)} %fusion.18, bf16[1536,128]{1,0:T(8,128)(2,1)S(1)} %reshape.261, bf16[]{:T(256)} %constant.12.clone.1), kind=kCustom, calls=%fused_computation.38 | custom fusion | bytes 393218 | tf_op jit(solution)/shard_map/scatter | solution.py:108
  154.8 5.4 %all-to-all-start.3 = ((bf16[64,24,128]{2,1,0:T(8,128)(2,1)}), bf16[64,24,128]{2,1,0:T(8,128)(2,1)S(1)}, u32[]{:S(2)}, u32[]{:S(2)}) async-start(bf16[64,24,128]{2,1,0:T(8,128)(2,1)} %bitcast.17), calls=%async_computation.3 | async-start | bytes 786432 | tf_op jit(solution)/shard_map/all_to_all | solution.py:114
  160.3 1.3 fusion.25
  161.6 1.3 fusion.23
  163.0 12.5 %all-to-all-done.3 = bf16[64,24,128]{2,1,0:T(8,128)(2,1)S(1)} async-done(((bf16[64,24,128]{2,1,0:T(8,128)(2,1)}), bf16[64,24,128]{2,1,0:T(8,128)(2,1)S(1)}, u32[]{:S(2)}, u32[]{:S(2)}) %all-to-all-start.3) | async-done | bytes 393248 | tf_op jit(solution)/shard_map/all_to_all | solution.py:114
  175.4 1.9 gather_fusion.4
  177.3 5.5 %fusion.2 = f32[3456,128]{1,0:T(8,128)} fusion(bf16[768,3456]{0,1:T(8,128)(2,1)} %bitcast.75, f32[768,128]{1,0:T(8,128)} %get-tuple-element.8, bf16[768,128]{1,0:T(8,128)(2,1)S(1)} %gather_fusion.4, pred[768]{0:T(1024)(128)(4,1)S(1)} %iota_compare_fusion.2, bf16[1,768,128]{2,1,0:T(8,128)(2,1)S(1)} %copy-done.4), kind=kOutput, calls=%fused_computation.24 | convolution fusion | flops 680853504 | bytes 7865088 | tf_op jit(solution)/shard_map/dot_general | solution.py:26
  182.9 0.3 convolution_convert_fusion.1
  183.1 0.2 reshape.245
  183.3 4.6 scatter_custom_fusion.1
  187.9 22.1 %all_to_all.20 = bf16[64,24,128]{2,1,0:T(8,128)(2,1)S(1)} all-to-all(bf16[64,24,128]{2,1,0:T(8,128)(2,1)S(1)} %bitcast.77), channel_id=1, replica_groups=mesh['scene'=4,'space'=64] {'space'}, dimensions={0} | all-to-all | bytes 786432 | tf_op jit(solution)/shard_map/all_to_all | solution.py:113
  210.0 1.9 gather_fusion.2
  211.9 0.8 fusion.1
  212.7 237.9 %all-reduce.4.cloned.1.call-done = (f32[3456,128]{1,0:T(8,128)}, f32[1024,256]{1,0:T(8,128)}, f32[256,1024]{1,0:T(8,128)}) async-done(((f32[3456,128]{1,0:T(8,128)}, f32[1024,256]{1,0:T(8,128)}, f32[256,1024]{1,0:T(8,128)}), (f32[3456,128]{1,0:T(8,128)}, f32[1024,256]{1,0:T(8,128)}, f32[256,1024]{1,0:T(8,128)})) %all-reduce.4.cloned.1.call-update) | async-done | bytes 3866640 | tf_op jit(solution)/shard_map/psum | solution.py:124
  450.6 2.9 copy.29
  453.5 2.3 copy.30
  455.7 1.0 copy.31
  (29 shorter events, 0.3 us)
Async XLA Ops:
  7.2 101.6 %copy-start = (bf16[3456,128]{1,0:T(8,128)(2,1)S(1)}, bf16[3456,128]{1,0:T(8,128)(2,1)}, u32[]{:S(2)}) copy-start(bf16[3456,128]{1,0:T(8,128)(2,1)} %param.11) | copy-start | bytes 2654212
  9.0 32.1 %collective-permute-start = (bf16[1,768,128]{2,1,0:T(8,128)(2,1)S(1)}, bf16[1,768,128]{2,1,0:T(8,128)(2,1)S(1)}, u32[]{:S(2)}, u32[]{:S(2)}) collective-permute-start(bf16[1,768,128]{2,1,0:T(8,128)(2,1)S(1)} %broadcast_select_fusion), channel_id=1, source_target_pairs={{0,1},{1,2},{2,3},{3,4},{4,5},{5,6},{6,7},{7,8},{8,9},{9,10},{10,1... | collective-permute-start | bytes 589832 | tf_op jit(solution)/shard_map/ppermute | solution.py:12
  13.5 27.6 %collective-permute-start.1 = (bf16[1,768,128]{2,1,0:T(8,128)(2,1)S(1)}, bf16[1,768,128]{2,1,0:T(8,128)(2,1)S(1)}, u32[]{:S(2)}, u32[]{:S(2)}) collective-permute-start(bf16[1,768,128]{2,1,0:T(8,128)(2,1)S(1)} %broadcast_select_fusion), channel_id=1, source_target_pairs={{1,0},{2,1},{3,2},{4,3},{5,4},{6,5},{7,6},{8,7},{9,8},{10,9},{11,1... | collective-permute-start | bytes 589832 | tf_op jit(solution)/shard_map/ppermute | solution.py:15
  25.1 93.5 %all-to-all-start.2 = ((bf16[64,24,128]{2,1,0:T(8,128)(2,1)}), bf16[64,24,128]{2,1,0:T(8,128)(2,1)S(1)}, u32[]{:S(2)}, u32[]{:S(2)}) async-start(bf16[64,24,128]{2,1,0:T(8,128)(2,1)} %bitcast.15), calls=%async_computation.2 | async-start | bytes 786432 | tf_op jit(solution)/shard_map/all_to_all | solution.py:89
  99.7 9.0 %copy-start.3 = (bf16[1,768,128]{2,1,0:T(8,128)(2,1)S(1)}, bf16[1,768,128]{2,1,0:T(8,128)(2,1)}, u32[]{:S(2)}) copy-start(bf16[1,768,128]{2,1,0:T(8,128)(2,1)} %param.9) | copy-start | bytes 589828
  108.7 20.2 %copy-start.5 = (s32[1,1,1536]{2,1,0:T(1,128)S(1)}, s32[1,1,1536]{2,1,0:T(1,128)}, u32[]{:S(2)}) copy-start(s32[1,1,1536]{2,1,0:T(1,128)} %param.17) | copy-start | bytes 18436
  113.6 33.8 %copy-start.1 = (bf16[1024,256]{1,0:T(8,128)(2,1)S(1)}, bf16[1024,256]{1,0:T(8,128)(2,1)}, u32[]{:S(2)}) copy-start(bf16[1024,256]{1,0:T(8,128)(2,1)} %param.12) | copy-start | bytes 1572868
  118.6 25.5 %all-to-all-start = ((bf16[64,24,128]{2,1,0:T(8,128)(2,1)}), bf16[64,24,128]{2,1,0:T(8,128)(2,1)S(1)}, u32[]{:S(2)}, u32[]{:S(2)}) async-start(bf16[64,24,128]{2,1,0:T(8,128)(2,1)} %bitcast.9), calls=%async_computation | async-start | bytes 786432 | tf_op jit(solution)/shard_map/all_to_all | solution.py:88
  147.4 29.9 %copy-start.4 = (bf16[1,768,128]{2,1,0:T(8,128)(2,1)S(1)}, bf16[1,768,128]{2,1,0:T(8,128)(2,1)}, u32[]{:S(2)}) copy-start(bf16[1,768,128]{2,1,0:T(8,128)(2,1)} %param.10) | copy-start | bytes 589828
  154.8 20.6 %all-to-all-start.3 = ((bf16[64,24,128]{2,1,0:T(8,128)(2,1)}), bf16[64,24,128]{2,1,0:T(8,128)(2,1)S(1)}, u32[]{:S(2)}, u32[]{:S(2)}) async-start(bf16[64,24,128]{2,1,0:T(8,128)(2,1)} %bitcast.17), calls=%async_computation.3 | async-start | bytes 786432 | tf_op jit(solution)/shard_map/all_to_all | solution.py:114
  160.3 290.3 %all-reduce.4.cloned.1.call-start = ((), (), s32[]{:S(2)}) async-start(), calls=%async_computation.4 | async-start | bytes 7733248 | tf_op jit(solution)/shard_map/psum | solution.py:124
  177.3 5.5 %copy-start.6 = (bf16[256,1024]{1,0:T(8,128)(2,1)S(1)}, bf16[256,1024]{1,0:T(8,128)(2,1)}, u32[]{:S(2)}) copy-start(bf16[256,1024]{1,0:T(8,128)(2,1)} %param.13) | copy-start | bytes 1572868
  450.6 5.2 %copy-start.2 = (f32[256,1024]{1,0:T(8,128)S(1)}, f32[256,1024]{1,0:T(8,128)}, u32[]{:S(2)}) copy-start(f32[256,1024]{1,0:T(8,128)} %get-tuple-element.12) | copy-start | bytes 3145732
Sparse Core Ops, SparseCore 0:
  183.0 267.5 all-reduce.3
where the time goes:
time: 465 us; the launch traced here: 464 us
  waiting for transfers between devices  262 us (56%)
  local copies, waits for them, and re-layouts  91.3 us (20%)
  starting transfers between devices  35.2 us (8%)
  other arithmetic  22.5 us (5%)
  blocking collectives  22.1 us (5%)
  matrix products  15.3 us (3%)
  between operations  15.1 us (3%)
    psum x1, waiting for transfers between devices, on_device(): lax.psum((grad_conv, grad_down, grad_up), ('scene', 'space'))  238 us
    gather x2, local copies, waits for them, and re-layouts, on_device(): rows = table[index]  49.5 us
    all_to_all x1, blocking collectives, on_device(): lax.all_to_all(unpack(up_rows), 'space', split_axis=0, concat_axis=0, til...  22.1 us
    all_to_all x1, starting transfers between devices, on_device(): lax.all_to_all(pack(grad_rows), 'space', split_axis=0, concat_axis=0, til...  13 us
    all_to_all x1, waiting for transfers between devices, on_device(): lax.all_to_all(unpack(grad_in), 'space', split_axis=0, concat_axis=0, til...  12.5 us
    all_to_all x1, waiting for transfers between devices, on_device(): lax.all_to_all(pack(mixed), 'space', split_axis=0, concat_axis=0, tiled=T...  11.7 us
    all_to_all x1, starting transfers between devices, on_device(): lax.all_to_all(pack(mixed), 'space', split_axis=0, concat_axis=0, tiled=T...  10.3 us
    scatter x2, local copies, waits for them, and re-layouts, unpack(): return jnp.zeros((2 * slots, width), jnp.bfloat16).at[order].set(rows.res...  9.73 us
  transfers between devices with their start and end apart: 6, of which 3 were waited for; matrix products, arithmetic and copies ran while one was open for 22% of the time, Pallas kernels for 0%

commit v1 on v0

--- a/solution.py
+++ b/solution.py
@@ -1,7 +1,206 @@
 import jax
 import jax.numpy as jnp
 from jax import lax
+from jax.experimental import pallas as pl
+from jax.experimental.pallas import tpu as pltpu
 from jax.sharding import PartitionSpec as P
+
+MESH = pl.DeviceIdType.MESH
+
+
+def place():
+    scene = lax.axis_index("scene")
+    space = lax.axis_index("space")
+    return scene, space // 8, (space // 2) % 4, space % 2
+
+
+def peer(y, z, x, c):
+    return {"scene": y, "space": (z * 4 + x) * 2 + c}
+
+
+def reduce_kernel(
+    src, out, send_c, recv_c, send_p, recv_p, send_z, recv_z, acc, sem_cs, sem_cr, sem_ps, sem_pr,
+    sem_zs, sem_zr, sem_gzs, sem_gzr, sem_gps, sem_gpr, sem_gcs, sem_gcr,
+):
+    y, z, x, c = place()
+    q = x * 4 + y
+    part = src.shape[2]
+    small = part // 8
+
+    def plane(k):
+        other = (q + k) % 16
+        return other, peer(other % 4, z, other // 4, c)
+
+    def column(k):
+        other = (z + k) % 8
+        return other, peer(y, other, x, c)
+
+    def rows(index):
+        return pl.ds(pl.multiple_of(index * small, small), small)
+
+    partner = peer(y, z, x, 1 - c)
+    barrier = pltpu.get_barrier_semaphore()
+    pl.semaphore_signal(barrier, inc=1, device_id=partner, device_id_type=MESH)
+
+    def greet_plane(k, carry):
+        pl.semaphore_signal(barrier, inc=1, device_id=plane(k)[1], device_id_type=MESH)
+        return carry
+
+    def greet_column(k, carry):
+        pl.semaphore_signal(barrier, inc=1, device_id=column(k)[1], device_id_type=MESH)
+        return carry
+
+    lax.fori_loop(1, 16, greet_plane, 0)
+    lax.fori_loop(1, 8, greet_column, 0)
+    pl.semaphore_wait(barrier, 23)
+
+    def core_copy(k):
+        return pltpu.make_async_remote_copy(
+            src_ref=send_c.at[k], dst_ref=recv_c.at[k], send_sem=sem_cs.at[k], recv_sem=sem_cr.at[k],
+            device_id=partner, device_id_type=MESH,
+        )
+
+    def plane_copy(k):
+        return pltpu.make_async_remote_copy(
+            src_ref=send_p.at[k], dst_ref=recv_p.at[k], send_sem=sem_ps.at[k], recv_sem=sem_pr.at[k],
+            device_id=plane(k)[1], device_id_type=MESH,
+        )
+
+    def column_copy(k):
+        return pltpu.make_async_remote_copy(
+            src_ref=send_z.at[k], dst_ref=recv_z.at[k], send_sem=sem_zs.at[k], recv_sem=sem_zr.at[k],
+            device_id=column(k)[1], device_id_type=MESH,
+        )
+
+    def to_core(j, carry):
+        k = (j + 1) % 16
+        send_c[k] = src[1 - c, plane(k)[0]].astype(jnp.bfloat16)
+        core_copy(k).start()
+        return carry
+
+    lax.fori_loop(0, 16, to_core, 0)
+
+    def to_plane(k, carry):
+        core_copy(k).wait_recv()
+        total = src[c, plane(k)[0]] + recv_c[k].astype(jnp.float32)
+        send_p[k] = total.astype(jnp.bfloat16)
+        plane_copy(k).start()
+        return carry
+
+    lax.fori_loop(1, 16, to_plane, 0)
+    core_copy(0).wait_recv()
+    acc[...] = src[c, q] + recv_c[0].astype(jnp.float32)
+
+    def add_plane(k, carry):
+        plane_copy(k).wait_recv()
+        acc[...] += recv_p[k].astype(jnp.float32)
+        return carry
+
+    lax.fori_loop(1, 16, add_plane, 0)
+
+    def to_column(k, carry):
+        send_z[k] = acc[rows(column(k)[0]), :].astype(jnp.bfloat16)
+        column_copy(k).start()
+        return carry
+
+    lax.fori_loop(1, 8, to_column, 0)
+
+    def add_column(k, total):
+        column_copy(k).wait_recv()
+        return total + recv_z[k].astype(jnp.float32)
+
+    total = lax.fori_loop(1, 8, add_column, acc[rows(z), :])
+    out[c, q, rows(z), :] = total.astype(jnp.bfloat16)
+
+    def gather_column(k, source):
+        piece = out.at[c, q, rows(source), :]
+        return pltpu.make_async_remote_copy(
+            src_ref=piece, dst_ref=piece, send_sem=sem_gzs.at[k], recv_sem=sem_gzr.at[k],
+            device_id=column(k)[1], device_id_type=MESH,
+        )
+
+    def gather_plane(k, source):
+        piece = out.at[c, source]
+        return pltpu.make_async_remote_copy(
+            src_ref=piece, dst_ref=piece, send_sem=sem_gps.at[k], recv_sem=sem_gpr.at[k],
+            device_id=plane(k)[1], device_id_type=MESH,
+        )
+
+    def gather_core(k, half):
+        piece = out.at[half, (q - k + 16) % 16]
+        return pltpu.make_async_remote_copy(
+            src_ref=piece, dst_ref=piece, send_sem=sem_gcs.at[k], recv_sem=sem_gcr.at[k],
+            device_id=partner, device_id_type=MESH,
+        )
+
+    def start_column(k, carry):
+        gather_column(k, z).start()
+        return carry
+
+    def wait_column(k, carry):
+        gather_column(k, (z - k + 8) % 8).wait_recv()
+        return carry
+
+    def start_plane(k, carry):
+        gather_plane(k, q).start()
+        return carry
+
+    def pass_core(k, carry):
+        gather_plane(k, (q - k + 16) % 16).wait_recv()
+        gather_core(k, c).start()
+        return carry
+
+    lax.fori_loop(1, 8, start_column, 0)
+    lax.fori_loop(1, 8, wait_column, 0)
+    lax.fori_loop(1, 16, start_plane, 0)
+    gather_core(0, c).start()
+    lax.fori_loop(1, 16, pass_core, 0)
+
+    def drain_core(k, carry):
+        gather_core(k, 1 - c).wait_recv()
+        gather_core(k, c).wait_send()
+        core_copy(k).wait_send()
+        return carry
+
+    def drain_plane(k, carry):
+        gather_plane(k, q).wait_send()
+        plane_copy(k).wait_send()
+        return carry
+
+    def drain_column(k, carry):
+        gather_column(k, z).wait_send()
+        column_copy(k).wait_send()
+        return carry
+
+    lax.fori_loop(0, 16, drain_core, 0)
+    lax.fori_loop(1, 16, drain_plane, 0)
+    lax.fori_loop(1, 8, drain_column, 0)
+
+
+def all_sum(block):
+    part = block.shape[2]
+    width = block.shape[3]
+    dma = pltpu.SemaphoreType.DMA
+    wire = jnp.bfloat16
+    return pl.pallas_call(
+        reduce_kernel,
+        out_shape=jax.ShapeDtypeStruct(block.shape, wire),
+        in_specs=[pl.BlockSpec(memory_space=pltpu.VMEM)],
+        out_specs=pl.BlockSpec(memory_space=pltpu.VMEM),
+        scratch_shapes=[
+            pltpu.VMEM((16, part, width), wire),
+            pltpu.VMEM((16, part, width), wire),
+            pltpu.VMEM((16, part, width), wire),
+            pltpu.VMEM((16, part, width), wire),
+            pltpu.VMEM((8, part // 8, width), wire),
+            pltpu.VMEM((8, part // 8, width), wire),
+            pltpu.VMEM((part, width), jnp.float32),
+            dma((16,)), dma((16,)), dma((16,)), dma((16,)), dma((8,)), dma((8,)),
+            dma((8,)), dma((8,)), dma((16,)), dma((16,)), dma((16,)), dma((16,)),
+        ],
+        compiler_params=pltpu.CompilerParams(collective_id=0, has_side_effects=True),
+        name="sum_gradients",
+    )(block)
 
 
 def extended(block, sides, width):
@@ -121,7 +320,18 @@
     grad_mixed = jnp.where(live, grad_rows.astype(jnp.float32) + fine_back.astype(jnp.float32), 0.0)
     grad_conv_pre = (grad_mixed * silu_grad(pre_conv)).astype(jnp.bfloat16)
     grad_conv = contract_rows(stacked, grad_conv_pre)
-    grad_conv, grad_down, grad_up = lax.psum((grad_conv, grad_down, grad_up), ("scene", "space"))
+    taps, wide = grad_conv.shape[0], grad_up.shape[0]
+    deep = grad_down.shape[0]
+    spare = jnp.zeros((deep * 4 - taps, width), jnp.float32)
+    down = grad_down.reshape(deep, wide // width, width).transpose(1, 0, 2).reshape(-1, width)
+    up = grad_up.reshape(wide, deep // width, width).transpose(1, 0, 2).reshape(-1, width)
+    block = jnp.concatenate([grad_conv, spare, down, up], axis=0)
+    total = all_sum(block.reshape(2, 16, -1, width)).reshape(-1, width)
+    grad_conv = total[:taps].astype(jnp.float32)
+    down = total[deep * 4 : deep * 4 + down.shape[0]].reshape(wide // width, deep, width)
+    up = total[deep * 4 + down.shape[0] * down.shape[1] :].reshape(deep // width, wide, width)
+    grad_down = down.transpose(1, 0, 2).reshape(deep, wide).astype(jnp.float32)
+    grad_up = up.transpose(1, 0, 2).reshape(wide, deep).astype(jnp.float32)
     return (output[None], grad_conv, grad_down, grad_up)
 
 

time: 465 us -> 258 us (0.55)
  waiting for transfers between devices: 262 us -> 16.1 us
  Pallas kernels: 0 us -> 58.8 us
  blocking collectives: 22.1 us -> 0 us
  between operations: 15.1 us -> 1.77 us
  other arithmetic: 22.5 us -> 34 us
  starting transfers between devices: 35.2 us -> 40.6 us
    psum x1 -> x0, waiting for transfers between devices: 238 us -> none  [on_device(): lax.psum((grad_conv, grad_down, grad_up), ('scene', 'space'))]
    pallas_call x0 -> x1, Pallas kernels: none -> 58.8 us  [all_sum(): pl.pallas_call(reduce_kernel, out_shape=jax.ShapeDtypeStruct(block.shape,...]
    all_to_all x1 -> x0, blocking collectives: 22.1 us -> none  [on_device(): lax.all_to_all(unpack(up_rows), 'space', split_axis=0, concat_axis=0, til...]
    concatenate x0 -> x1, other arithmetic: none -> 8.98 us  [on_device(): block = jnp.concatenate([grad_conv, spare, down, up], axis=0)]
    all_to_all x1, waiting for transfers between devices: 12.5 us -> 5.84 us  [on_device(): lax.all_to_all(unpack(grad_in), 'space', split_axis=0, concat_axis=0, til...]
    all_to_all x0 -> x1, starting transfers between devices: none -> 5.46 us  [on_device(): lax.all_to_all(unpack(up_rows), 'space', split_axis=0, concat_axis=0, til...]
  transfers between devices with their start and end apart: 6 -> 6, of which waited for: 3 -> 2; matrix products, arithmetic and copies ran while one was open for 22% -> 49% of each run, Pallas kernels for 0% -> 23%
where the time goes in v1:
time: 258 us; the launch traced here: 257 us
  local copies, waits for them, and re-layouts  90.4 us (35%)
  Pallas kernels  58.8 us (23%)
  starting transfers between devices  40.6 us (16%)
  other arithmetic  34 us (13%)
  waiting for transfers between devices  16.1 us (6%)
  matrix products  15.1 us (6%)
    pallas_call x1, Pallas kernels, all_sum(): pl.pallas_call(reduce_kernel, out_shape=jax.ShapeDtypeStruct(block.shape,...  58.8 us
    gather x2, local copies, waits for them, and re-layouts, on_device(): rows = table[index]  49.5 us
    all_to_all x1, starting transfers between devices, on_device(): lax.all_to_all(pack(grad_rows), 'space', split_axis=0, concat_axis=0, til...  13 us
    scatter x2, local copies, waits for them, and re-layouts, unpack(): return jnp.zeros((2 * slots, width), jnp.bfloat16).at[order].set(rows.res...  10.4 us
    all_to_all x1, starting transfers between devices, on_device(): lax.all_to_all(pack(mixed), 'space', split_axis=0, concat_axis=0, tiled=T...  10.3 us
    all_to_all x1, waiting for transfers between devices, on_device(): lax.all_to_all(pack(mixed), 'space', split_axis=0, concat_axis=0, tiled=T...  10.3 us
    concatenate x1, local copies, waits for them, and re-layouts, on_device(): jnp.concatenate([own[:, None, :], rows], axis=1).reshape(slots, 27 * width)  9 us
    concatenate x1, other arithmetic, on_device(): block = jnp.concatenate([grad_conv, spare, down, up], axis=0)  8.98 us
  transfers between devices with their start and end apart: 6, of which 2 were waited for; matrix products, arithmetic and copies ran while one was open for 49% of the time, Pallas kernels for 23%

profile of v1, /device:TPU:1, one launch (start us, length us, event | category | flops | bytes accessed | tf_op | source)
XLA Modules:
  0.0 256.8 jit_solution(8898775069151182496)
XLA Ops:
  1.4 1.1 broadcast_select_fusion
  2.5 4.5 %collective-permute-start = (bf16[1,768,128]{2,1,0:T(8,128)(2,1)S(1)}, bf16[1,768,128]{2,1,0:T(8,128)(2,1)S(1)}, u32[]{:S(2)}, u32[]{:S(2)}) collective-permute-start(bf16[1,768,128]{2,1,0:T(8,128)(2,1)S(1)} %broadcast_select_fusion), channel_id=1, source_target_pairs={{0,1},{1,2},{2,3},{3,4},{4,5},{5,6},{6,7},{7,8},{8,9},{9,10},{10,1... | collective-permute-start | bytes 589832 | tf_op jit(solution)/shard_map/ppermute | solution.py:211
  7.0 1.9 collective-permute-start.1
  8.9 0.7 reduce.1
  9.6 1.8 reduce-window.6
  11.4 0.3 slice_reduce_fusion
  11.9 0.7 fusion.34
  12.6 6.0 %scatter_custom_fusion.2 = bf16[1536,128]{1,0:T(8,128)(2,1)} fusion(s32[768]{0:T(1024)S(1)} %fusion.34, bf16[]{:T(256)} %constant.12.clone.1, bf16[1,768,128]{2,1,0:T(8,128)(2,1)} %param.10, pred[768]{0:T(1024)(128)(4,1)S(1)} %iota_compare_fusion.2), kind=kCustom, calls=%fused_computation.55 | custom fusion | flops 98304 | bytes 591872 | tf_op jit(solution)/shard_map/scatter | solution.py:265
  18.6 13.0 %all-to-all-start.2 = ((bf16[64,24,128]{2,1,0:T(8,128)(2,1)}), bf16[64,24,128]{2,1,0:T(8,128)(2,1)S(1)}, u32[]{:S(2)}, u32[]{:S(2)}) async-start(bf16[64,24,128]{2,1,0:T(8,128)(2,1)} %bitcast.15), calls=%async_computation.2 | async-start | bytes 786432 | tf_op jit(solution)/shard_map/all_to_all | solution.py:288
  31.6 1.1 bitcast_select_fusion.1
  32.7 1.1 compare_select_fusion.2
  33.8 0.2 copy.24
  34.0 0.3 reshape.231
  34.3 0.3 copy.25
  34.8 40.5 %gather_fusion = bf16[19968,128]{1,0:T(8,128)(2,1)} fusion(bf16[2305,128]{1,0:T(8,128)(2,1)S(1)} %concatenate.13, s32[20480]{0:T(1024)S(1)} %pad_clamp_fusion), kind=kCustom, calls=%fused_computation | custom fusion | bytes 10303488 | tf_op jit(solution)/shard_map/gather | solution.py:279
  75.2 9.1 %reshape.230 = bf16[768,26,128]{2,1,0:T(8,128)(2,1)} reshape(bf16[19968,128]{1,0:T(8,128)(2,1)} %gather_fusion) | data formatting | bytes 10223616 | tf_op jit(solution)/shard_map/gather | solution.py:279
  84.3 8.9 %pad_maximum_fusion = bf16[768,27,128]{2,1,0:T(8,128)(2,1)} fusion(bf16[768,26,128]{2,1,0:T(8,128)(2,1)} %reshape.230, bf16[768,1,128]{2,1,0:T(2,128)(2,1)S(1)} %copy.25), kind=kLoop, calls=%fused_computation.9 | loop fusion | flops 10616832 | bytes 10616832 | tf_op jit(solution)/shard_map/concatenate | solution.py:280
  93.2 9.0 %copy.26 = bf16[768,27,128]{0,2,1:T(8,128)(2,1)} copy(bf16[768,27,128]{2,1,0:T(8,128)(2,1)} %pad_maximum_fusion) | data formatting | bytes 10616832 | tf_op jit(solution)/shard_map/concatenate | solution.py:280
  102.2 4.9 %select_convert_fusion.1 = (bf16[768,128]{1,0:T(8,128)(2,1)S(1)}, f32[768,128]{1,0:T(8,128)}) fusion(bf16[1,768,128]{2,1,0:T(8,128)(2,1)S(1)} %copy-done.2, pred[768]{0:T(1024)(128)(4,1)S(1)} %iota_compare_fusion.2, bf16[768,3456]{0,1:T(8,128)(2,1)} %bitcast.143, bf16[3456,128]{1,0:T(8,128)(2,1)S(1)} %copy-done), kind=kOutput, calls=%fused_computation.22 | convolution fusion | flops 680361984 | bytes 6980352 | tf_op jit(solution)/shard_map/dot_general | solution.py:281
  107.1 5.0 %scatter_custom_fusion = bf16[1536,128]{1,0:T(8,128)(2,1)} fusion(s32[768]{0:T(1024)S(1)} %fusion.34, bf16[768,128]{1,0:T(8,128)(2,1)S(1)} %get-tuple-element.6, bf16[]{:T(256)} %constant.12.clone.1), kind=kCustom, calls=%fused_computation.59 | custom fusion | bytes 393218 | tf_op jit(solution)/shard_map/scatter | solution.py:265
  112.0 10.3 %all-to-all-start = ((bf16[64,24,128]{2,1,0:T(8,128)(2,1)}), bf16[64,24,128]{2,1,0:T(8,128)(2,1)S(1)}, u32[]{:S(2)}, u32[]{:S(2)}) async-start(bf16[64,24,128]{2,1,0:T(8,128)(2,1)} %bitcast.9), calls=%async_computation | async-start | bytes 786432 | tf_op jit(solution)/shard_map/all_to_all | solution.py:287
  122.5 3.2 %gather_fusion.3 = bf16[1536,128]{1,0:T(8,128)(2,1)S(1)} fusion(bf16[1536,128]{1,0:T(8,128)(2,1)S(1)} %bitcast.136, s32[2048]{0:T(1024)S(1)} %pad_clamp_fusion.1), kind=kCustom, calls=%fused_computation.3 | custom fusion | bytes 792576 | tf_op jit(solution)/shard_map/gather | solution.py:293
  125.7 0.2 reshape.215
  125.9 1.4 fusion.41
  127.2 10.3 %all-to-all-done = bf16[64,24,128]{2,1,0:T(8,128)(2,1)S(1)} async-done(((bf16[64,24,128]{2,1,0:T(8,128)(2,1)}), bf16[64,24,128]{2,1,0:T(8,128)(2,1)S(1)}, u32[]{:S(2)}, u32[]{:S(2)}) %all-to-all-start) | async-done | bytes 393248 | tf_op jit(solution)/shard_map/all_to_all | solution.py:287
  137.5 3.2 %gather_fusion.1 = bf16[1536,128]{1,0:T(8,128)(2,1)S(1)} fusion(bf16[1536,128]{1,0:T(8,128)(2,1)S(1)} %bitcast.137, s32[2048]{0:T(1024)S(1)} %pad_clamp_fusion.1), kind=kCustom, calls=%fused_computation.1 | custom fusion | bytes 792576 | tf_op jit(solution)/shard_map/gather | solution.py:292
  141.1 0.3 fusion.40
  141.4 0.3 convolution_convert_fusion
  141.9 5.2 %scatter_custom_fusion.3 = bf16[1536,128]{1,0:T(8,128)(2,1)} fusion(s32[1536]{0:T(1024)S(1)} %fusion.33, bf16[1536,128]{1,0:T(8,128)(2,1)S(1)} %reshape.297, bf16[]{:T(256)} %constant.12.clone.1), kind=kCustom, calls=%fused_computation.53 | custom fusion | bytes 393218 | tf_op jit(solution)/shard_map/scatter | solution.py:307
  147.1 5.4 %all-to-all-start.3 = ((bf16[64,24,128]{2,1,0:T(8,128)(2,1)}), bf16[64,24,128]{2,1,0:T(8,128)(2,1)S(1)}, u32[]{:S(2)}, u32[]{:S(2)}) async-start(bf16[64,24,128]{2,1,0:T(8,128)(2,1)} %bitcast.17), calls=%async_computation.3 | async-start | bytes 786432 | tf_op jit(solution)/shard_map/all_to_all | solution.py:313
  152.5 1.3 convolution_convert_fusion.1
  154.0 5.2 %scatter_custom_fusion.1 = bf16[1536,128]{1,0:T(8,128)(2,1)} fusion(s32[1536]{0:T(1024)S(1)} %fusion.33, bf16[1536,128]{1,0:T(8,128)(2,1)S(1)} %reshape.281, bf16[]{:T(256)} %constant.12.clone.1), kind=kCustom, calls=%fused_computation.57 | custom fusion | bytes 393218 | tf_op jit(solution)/shard_map/scatter | solution.py:307
  159.2 0.3 fusion
  159.6 2.3 fusion.27
  161.8 5.8 %all-to-all-done.3 = bf16[64,24,128]{2,1,0:T(8,128)(2,1)S(1)} async-done(((bf16[64,24,128]{2,1,0:T(8,128)(2,1)}), bf16[64,24,128]{2,1,0:T(8,128)(2,1)S(1)}, u32[]{:S(2)}, u32[]{:S(2)}) %all-to-all-start.3) | async-done | bytes 393248 | tf_op jit(solution)/shard_map/all_to_all | solution.py:313
  167.7 5.5 %all-to-all-start.1 = ((bf16[64,24,128]{2,1,0:T(8,128)(2,1)}), bf16[64,24,128]{2,1,0:T(8,128)(2,1)S(1)}, u32[]{:S(2)}, u32[]{:S(2)}) async-start(bf16[64,24,128]{2,1,0:T(8,128)(2,1)} %bitcast.11), calls=%async_computation.1 | async-start | bytes 786432 | tf_op jit(solution)/shard_map/all_to_all | solution.py:312
  173.1 1.9 gather_fusion.4
  175.0 4.4 %fusion.4 = f32[3456,128]{1,0:T(8,128)S(1)} fusion(bf16[768,3456]{0,1:T(8,128)(2,1)} %bitcast.144, f32[768,128]{1,0:T(8,128)} %get-tuple-element.7, bf16[768,128]{1,0:T(8,128)(2,1)S(1)} %gather_fusion.4, pred[768]{0:T(1024)(128)(4,1)S(1)} %iota_compare_fusion.2, bf16[1,768,128]{2,1,0:T(8,128)(2,1)} %param.10), kind=kOutput, calls=%fused_computation.29 | convolution fusion | flops 680853504 | bytes 7865088 | tf_op jit(solution)/shard_map/dot_general | solution.py:225
  179.4 9.0 %pad_maximum_fusion.1 = f32[8192,128]{1,0:T(8,128)} fusion(f32[2048,128]{1,0:T(8,128)S(1)} %bitcast.147, f32[2048,128]{1,0:T(8,128)S(1)} %bitcast.153, f32[3456,128]{1,0:T(8,128)S(1)} %fusion.4, f32[8192]{0:T(1024)S(1)} %pad.2.clone), kind=kLoop, calls=%fused_computation.10 | loop fusion | flops 3145728 | bytes 8093696 | tf_op jit(solution)/shard_map/concatenate | solution.py:328
  188.4 58.8 %sum_gradients.1 = bf16[2,16,256,128]{3,2,1,0:T(8,128)(2,1)} custom-call(f32[2,16,256,128]{3,2,1,0:T(8,128)} %bitcast.138), custom_call_target="tpu_custom_call" | custom-call | tf_op jit(solution)/shard_map/sum_gradients/pallas_call | solution.py:185
  247.2 1.3 fusion.39
  248.5 0.3 copy.31
  248.8 1.2 copy.50
  250.0 0.5 copy.30
  250.5 1.0 copy.51
  251.6 2.5 slice_convert_fusion
  254.1 1.9 gather_fusion.2
  255.9 0.8 fusion.3
  (37 shorter events, 1.1 us)
Async XLA Ops:
  0.6 101.6 %copy-start = (bf16[3456,128]{1,0:T(8,128)(2,1)S(1)}, bf16[3456,128]{1,0:T(8,128)(2,1)}, u32[]{:S(2)}) copy-start(bf16[3456,128]{1,0:T(8,128)(2,1)} %param.11) | copy-start | bytes 2654212
  2.5 32.1 %collective-permute-start = (bf16[1,768,128]{2,1,0:T(8,128)(2,1)S(1)}, bf16[1,768,128]{2,1,0:T(8,128)(2,1)S(1)}, u32[]{:S(2)}, u32[]{:S(2)}) collective-permute-start(bf16[1,768,128]{2,1,0:T(8,128)(2,1)S(1)} %broadcast_select_fusion), channel_id=1, source_target_pairs={{0,1},{1,2},{2,3},{3,4},{4,5},{5,6},{6,7},{7,8},{8,9},{9,10},{10,1... | collective-permute-start | bytes 589832 | tf_op jit(solution)/shard_map/ppermute | solution.py:211
  7.0 27.6 %collective-permute-start.1 = (bf16[1,768,128]{2,1,0:T(8,128)(2,1)S(1)}, bf16[1,768,128]{2,1,0:T(8,128)(2,1)S(1)}, u32[]{:S(2)}, u32[]{:S(2)}) collective-permute-start(bf16[1,768,128]{2,1,0:T(8,128)(2,1)S(1)} %broadcast_select_fusion), channel_id=1, source_target_pairs={{1,0},{2,1},{3,2},{4,3},{5,4},{6,5},{7,6},{8,7},{9,8},{10,9},{11,1... | collective-permute-start | bytes 589832 | tf_op jit(solution)/shard_map/ppermute | solution.py:214
  18.6 93.5 %all-to-all-start.2 = ((bf16[64,24,128]{2,1,0:T(8,128)(2,1)}), bf16[64,24,128]{2,1,0:T(8,128)(2,1)S(1)}, u32[]{:S(2)}, u32[]{:S(2)}) async-start(bf16[64,24,128]{2,1,0:T(8,128)(2,1)} %bitcast.15), calls=%async_computation.2 | async-start | bytes 786432 | tf_op jit(solution)/shard_map/all_to_all | solution.py:288
  93.2 9.0 %copy-start.2 = (bf16[1,768,128]{2,1,0:T(8,128)(2,1)S(1)}, bf16[1,768,128]{2,1,0:T(8,128)(2,1)}, u32[]{:S(2)}) copy-start(bf16[1,768,128]{2,1,0:T(8,128)(2,1)} %param.9) | copy-start | bytes 589828
  102.2 20.2 %copy-start.7 = (s32[1,1,1536]{2,1,0:T(1,128)S(1)}, s32[1,1,1536]{2,1,0:T(1,128)}, u32[]{:S(2)}) copy-start(s32[1,1,1536]{2,1,0:T(1,128)} %param.17) | copy-start | bytes 18436
  107.1 5.0 %copy-start.4 = (bf16[768,128]{1,0:T(8,128)(2,1)}, bf16[768,128]{1,0:T(8,128)(2,1)S(1)}, u32[]{:S(2)}) copy-start(bf16[768,128]{1,0:T(8,128)(2,1)S(1)} %get-tuple-element.6) | copy-start | bytes 589828
  112.0 25.5 %all-to-all-start = ((bf16[64,24,128]{2,1,0:T(8,128)(2,1)}), bf16[64,24,128]{2,1,0:T(8,128)(2,1)S(1)}, u32[]{:S(2)}, u32[]{:S(2)}) async-start(bf16[64,24,128]{2,1,0:T(8,128)(2,1)} %bitcast.9), calls=%async_computation | async-start | bytes 786432 | tf_op jit(solution)/shard_map/all_to_all | solution.py:287
  122.4 18.7 %copy-start.3 = (bf16[1024,256]{1,0:T(8,128)(2,1)S(1)}, bf16[1024,256]{1,0:T(8,128)(2,1)}, u32[]{:S(2)}) copy-start(bf16[1024,256]{1,0:T(8,128)(2,1)} %param.12) | copy-start | bytes 1572868
  127.2 25.3 %copy-start.6 = (f32[192,256]{1,0:T(8,128)}, f32[192,256]{1,0:T(8,128)S(1)}, u32[]{:S(2)}) copy-start(f32[192,256]{1,0:T(8,128)S(1)} %fusion.41) | copy-start | bytes 589828
  147.1 20.6 %all-to-all-start.3 = ((bf16[64,24,128]{2,1,0:T(8,128)(2,1)}), bf16[64,24,128]{2,1,0:T(8,128)(2,1)S(1)}, u32[]{:S(2)}, u32[]{:S(2)}) async-start(bf16[64,24,128]{2,1,0:T(8,128)(2,1)} %bitcast.17), calls=%async_computation.3 | async-start | bytes 786432 | tf_op jit(solution)/shard_map/all_to_all | solution.py:313
  167.7 86.4 %all-to-all-start.1 = ((bf16[64,24,128]{2,1,0:T(8,128)(2,1)}), bf16[64,24,128]{2,1,0:T(8,128)(2,1)S(1)}, u32[]{:S(2)}, u32[]{:S(2)}) async-start(bf16[64,24,128]{2,1,0:T(8,128)(2,1)} %bitcast.11), calls=%async_computation.1 | async-start | bytes 786432 | tf_op jit(solution)/shard_map/all_to_all | solution.py:312
  175.0 4.4 %copy-start.1 = (f32[1024,2,128]{2,0,1:T(8,128)S(1)}, f32[1024,2,128]{2,0,1:T(8,128)}, u32[]{:S(2)}) copy-start(f32[1024,2,128]{2,0,1:T(8,128)} %fusion.27) | copy-start | bytes 3145732
  248.8 7.1 %copy-start.5 = (bf16[768,128]{1,0:T(8,128)(2,1)S(1)}, bf16[768,128]{1,0:T(8,128)(2,1)}, u32[]{:S(2)}) copy-start(bf16[768,128]{1,0:T(8,128)(2,1)} %copy-done.4) | copy-start | bytes 589828

commit v2 on v1

--- a/solution.py
+++ b/solution.py
@@ -4,6 +4,11 @@
 from jax.experimental import pallas as pl
 from jax.experimental.pallas import tpu as pltpu
 from jax.sharding import PartitionSpec as P
+
+def silu_grad(value):
+    sigma = jax.nn.sigmoid(value)
+    return sigma * (1.0 + value * (1.0 - sigma))
+
 
 MESH = pl.DeviceIdType.MESH
 
@@ -203,133 +208,364 @@
     )(block)
 
 
-def extended(block, sides, width):
-    for axis, dim in sides:
-        count = lax.axis_size(axis)
-        forward = [(i, i + 1) for i in range(count - 1)]
-        backward = [(target, source) for source, target in forward]
-        low = lax.ppermute(
-            lax.slice_in_dim(block, block.shape[dim] - width, None, axis=dim), axis, forward
-        )
-        high = lax.ppermute(lax.slice_in_dim(block, 0, width, axis=dim), axis, backward)
-        block = jnp.concatenate([low, block, high], axis=dim)
-    return block
-
-
-def silu_grad(value):
-    sigma = jax.nn.sigmoid(value)
-    return sigma * (1.0 + value * (1.0 - sigma))
-
-
-def contract_rows(left, right):
+def one_hot(condition):
+    return jnp.where(condition, 1.0, 0.0).astype(jnp.bfloat16)
+
+
+def iota(shape, axis):
+    return lax.broadcasted_iota(jnp.int32, shape, axis)
+
+
+def dot(left, right, left_axis=1, right_axis=0):
     return lax.dot_general(
-        left, right, (((0,), (0,)), ((), ())), preferred_element_type=jnp.float32
+        left, right, (((left_axis,), (right_axis,)), ((), ())), preferred_element_type=jnp.float32
     )
 
 
-def contract_cols(left, right):
-    return lax.dot_general(
-        left, right, (((1,), (1,)), ((), ())), preferred_element_type=jnp.float32
+def step_kernel(
+    features, cotangent, conv_weight, down_weight, up_weight, live_count, codes, dest, order,
+    output, block,
+    own, grads, table, weight_t, stacked, pre_fine, mixed, rim, target_row, target_col, order_col,
+    send_m, recv_m, send_g, recv_g, send_u, recv_u, joined, coarse_in, coarse_grad, returned, slope,
+    sem_rs, sem_rr, sem_ms, sem_mr, sem_gs, sem_gr, sem_us, sem_ur,
+):
+    y, z, x, c = place()
+    me = (z * 4 + x) * 2 + c
+    slots, width = features.shape
+    edge = slots // 8
+    places, cap = send_m.shape[0], send_m.shape[1]
+    group = 8
+    span = group * cap
+    bricks = coarse_in.shape[0]
+    taps = codes.shape[0]
+
+    def at(device):
+        return {"scene": y, "space": device}
+
+    rim[...] = jnp.zeros_like(rim)
+    barrier = pltpu.get_barrier_semaphore()
+
+    def greet(k, carry):
+        pl.semaphore_signal(
+            barrier, inc=1, device_id=at((me + k) % places), device_id_type=MESH
+        )
+        return carry
+
+    lax.fori_loop(1, places, greet, 0)
+
+    count = live_count[0, 0]
+    live = iota((slots, width), 0) < count
+    zero_b = jnp.zeros((slots, width), jnp.bfloat16)
+    own[...] = jnp.where(live, features[...], zero_b)
+    grads[...] = jnp.where(live, cotangent[...], zero_b)
+
+    goal = dest[...]
+    named = goal == iota((places, slots), 0)
+    named_b = one_hot(named)
+    for part in range(3):
+        cols = slice(part * 256, part * 256 + 256)
+        earlier = one_hot(iota((slots, 256), 0) < iota((slots, 256), 1) + part * 256)
+        before = dot(named_b, earlier)
+        rank = jnp.sum(jnp.where(named[:, cols], before, 0.0), axis=0, keepdims=True)
+        row = goal[:, cols].astype(jnp.float32) * cap + rank
+        target_row[:, cols] = row
+        target_col[cols, :] = jnp.broadcast_to(row, (128, 256)).T
+
+    for part in range(12):
+        cols = slice(part * 128, part * 128 + 128)
+        order_col[cols, :] = jnp.broadcast_to(order[:, cols].astype(jnp.float32), (128, 128)).T
+
+    pl.semaphore_wait(barrier, places - 1)
+
+    def rim_copy(upward):
+        start = edge if upward else 0
+        there = 0 if upward else edge
+        return pltpu.make_async_remote_copy(
+            src_ref=features.at[pl.ds(start, edge), :], dst_ref=rim.at[pl.ds(there, edge), :],
+            send_sem=sem_rs.at[1 - int(upward)], recv_sem=sem_rr.at[1 - int(upward)],
+            device_id=at((me + (1 if upward else places - 1)) % places), device_id_type=MESH,
+        )
+
+    @pl.when(me < places - 1)
+    def _():
+        rim_copy(True).start()
+
+    @pl.when(me > 0)
+    def _():
+        rim_copy(False).start()
+
+    def exchange(sent, received, send_sems, recv_sems, device, source):
+        return pltpu.make_async_remote_copy(
+            src_ref=sent.at[device], dst_ref=received.at[source],
+            send_sem=send_sems.at[device], recv_sem=recv_sems.at[source],
+            device_id=at(device), device_id_type=MESH,
+        )
+
+    def send_group(which, sent, received, send_sems, recv_sems):
+        def one(k, carry):
+            device = which * group + (me + k) % group
+
+            @pl.when(device != me)
+            def _():
+                exchange(sent, received, send_sems, recv_sems, device, me).start()
+
+            return carry
+
+        lax.fori_loop(0, group, one, 0)
+
+    def in_order(j):
+        odd = j % 2
+        return (z + 4 - odd + (1 - 2 * odd) * (j // 2)) % 8
+
+    def spread(rows, sent, received, send_sems, recv_sems):
+        def one(j, carry):
+            which = in_order(j)
+            chosen = one_hot(
+                (iota((span, slots), 0) + which * span).astype(jnp.float32) == target_row[...]
+            )
+            packed = dot(chosen, rows[...]).reshape(group, cap, width).astype(jnp.bfloat16)
+            sent[pl.ds(which * group, group)] = packed
+            send_group(which, sent, received, send_sems, recv_sems)
+            return carry
+
+        lax.fori_loop(0, places // group, one, 0)
+        received[pl.ds(me, 1)] = sent[pl.ds(me, 1)]
+
+    spread(grads, send_g, recv_g, sem_gs, sem_gr)
+
+    def turn(k, carry):
+        rows = pl.ds(pl.multiple_of(k * width, width), width)
+        weight_t[:, rows] = conv_weight[rows, :].astype(jnp.float32).T.astype(jnp.bfloat16)
+        return carry
+
+    lax.fori_loop(0, taps + 1, turn, 0)
+    for part in range(6):
+        cols = slice(part * 128, part * 128 + 128)
+        turned = own[cols, :].astype(jnp.float32).T.astype(jnp.bfloat16)
+        table[:, cols] = turned
+        stacked[0:width, cols] = turned
+
+    def pick(k, part, depth):
+        code = codes[pl.ds(k, 1), part * 256 : part * 256 + 256]
+        chosen = one_hot(iota((depth, 256), 0) == code)
+        found = dot(table[:, 0:depth], chosen).astype(jnp.bfloat16)
+        rows = pl.ds(pl.multiple_of((k + 1) * width, width), width)
+        stacked[rows, part * 256 : part * 256 + 256] = found
+
+    def inner(k, carry):
+        pick(k, 1, slots)
+        pick(k, 2, slots)
+        return carry
+
+    lax.fori_loop(0, taps, inner, 0)
+
+    @pl.when(me > 0)
+    def _():
+        rim_copy(True).wait_recv()
+
+    @pl.when(me < places - 1)
+    def _():
+        rim_copy(False).wait_recv()
+
+    table[:, slots:] = rim[...].astype(jnp.float32).T.astype(jnp.bfloat16)
+
+    def outer(k, carry):
+        pick(k, 0, slots + 256)
+        return carry
+
+    lax.fori_loop(0, taps, outer, 0)
+
+    for part in range(3):
+        cols = slice(part * 256, part * 256 + 256)
+        pre = dot(weight_t[...], stacked[:, cols]).T
+        pre_fine[cols, :] = pre
+        alive = iota((256, width), 0) + part * 256 < count
+        blend = jnp.where(alive, own[cols, :].astype(jnp.float32) + jax.nn.silu(pre), 0.0)
+        mixed[cols, :] = blend.astype(jnp.bfloat16)
+
+    spread(mixed, send_m, recv_m, sem_ms, sem_mr)
+
+    def arrived(received, sent, send_sems, recv_sems):
+        def one(k, carry):
+            exchange(sent, received, send_sems, recv_sems, me, (me + k) % places).wait_recv()
+            return carry
+
+        lax.fori_loop(1, places, one, 0)
+
+    def left(received, sent, send_sems, recv_sems):
+        def one(k, carry):
+            exchange(sent, received, send_sems, recv_sems, (me + k) % places, me).wait_send()
+            return carry
+
+        lax.fori_loop(1, places, one, 0)
+
+    def flat(received, lanes, base):
+        def one(j, carry):
+            rows = pl.ds(pl.multiple_of(j * span, span), span)
+            value = received[pl.ds(j * group, group)].astype(jnp.float32)
+            joined[rows, base : base + lanes] = value.reshape(span, lanes).astype(jnp.bfloat16)
+            return carry
+
+        lax.fori_loop(0, places // group, one, 0)
+
+    arrived(recv_g, send_g, sem_gs, sem_gr)
+    flat(recv_g, width, width)
+    arrived(recv_m, send_m, sem_ms, sem_mr)
+    flat(recv_m, width, 0)
+
+    received_rows = places * cap
+
+    def bring(k, carry):
+        rows = pl.ds(pl.multiple_of(k * bricks, bricks), bricks)
+        cols = pl.ds(pl.multiple_of(k * width, width), width)
+        chosen = one_hot(
+            order_col[rows, 0:1] == iota((bricks, received_rows), 1).astype(jnp.float32)
+        )
+        pair = dot(chosen, joined[...]).astype(jnp.bfloat16)
+        coarse_in[:, cols] = pair[:, 0:width]
+        coarse_grad[:, cols] = pair[:, width:]
+        return carry
+
+    lax.fori_loop(0, 8, bring, 0)
+
+    pre = dot(coarse_in[...], down_weight[...])
+    coarse = jax.nn.silu(pre).astype(jnp.bfloat16)
+    back = dot(coarse_grad[...], up_weight[...], 1, 1)
+    grad_pre = (back * silu_grad(pre)).astype(jnp.bfloat16)
+    up_rows = dot(coarse, up_weight[...]).astype(jnp.bfloat16)
+    grad_in = dot(grad_pre, down_weight[...], 1, 1).astype(jnp.bfloat16)
+    for k in range(8):
+        rows = slice(k * bricks, k * bricks + bricks)
+        returned[rows, 0:width] = up_rows[:, k * width : k * width + width]
+        returned[rows, width:] = grad_in[:, k * width : k * width + width]
+
+    def give(j, carry):
+        which = in_order(j)
+        chosen = one_hot(iota((span, received_rows), 0) + which * span == order[...])
+        packed = dot(chosen, returned[...]).reshape(group, cap, 2 * width).astype(jnp.bfloat16)
+        send_u[pl.ds(which * group, group)] = packed
+        send_group(which, send_u, recv_u, sem_us, sem_ur)
+        return carry
+
+    lax.fori_loop(0, places // group, give, 0)
+    recv_u[pl.ds(me, 1)] = send_u[pl.ds(me, 1)]
+
+    deep, wide = down_weight.shape
+    base = 4 * deep
+    grad_down = dot(coarse_in[...], grad_pre, 0, 0)
+    for k in range(wide // width):
+        block[base + k * deep : base + (k + 1) * deep, :] = grad_down[:, k * width : k * width + width]
+    base = base + deep * wide // width
+    grad_up = dot(coarse, coarse_grad[...], 0, 0)
+    for k in range(deep // width):
+        block[base + k * wide : base + (k + 1) * wide, :] = grad_up[:, k * width : k * width + width]
+
+    arrived(recv_u, send_u, sem_us, sem_ur)
+    flat(recv_u, 2 * width, 0)
+
+    def settle(part, carry):
+        rows = pl.ds(pl.multiple_of(part * 256, 256), 256)
+        chosen = one_hot(
+            target_col[rows, 0:1] == iota((256, received_rows), 1).astype(jnp.float32)
+        )
+        fine = dot(chosen, joined[...])
+        alive = iota((256, width), 0) + part * 256 < count
+        total = mixed[rows, :].astype(jnp.float32) + fine[:, 0:width]
+        output[rows, :] = jnp.where(alive, total, 0.0).astype(jnp.bfloat16)
+        grad_mixed = jnp.where(alive, grads[rows, :].astype(jnp.float32) + fine[:, width:], 0.0)
+        slope[rows, :] = (grad_mixed * silu_grad(pre_fine[rows, :])).astype(jnp.bfloat16)
+        return carry
+
+    lax.fori_loop(0, 3, settle, 0)
+
+    def convolve(k, carry):
+        rows = pl.ds(pl.multiple_of(k * 384, 384), 384)
+        block[rows, :] = dot(stacked[rows, :], slope[...])
+        return carry
+
+    lax.fori_loop(0, 9, convolve, 0)
+    block[27 * width : 4 * deep, :] = jnp.zeros((4 * deep - 27 * width, width), jnp.float32)
+
+    left(recv_g, send_g, sem_gs, sem_gr)
+    left(recv_m, send_m, sem_ms, sem_mr)
+    left(recv_u, send_u, sem_us, sem_ur)
+
+    @pl.when(me < places - 1)
+    def _():
+        rim_copy(True).wait_send()
+
+    @pl.when(me > 0)
+    def _():
+        rim_copy(False).wait_send()
+
+
+def whole_step(features, cotangent, conv_weight, down_weight, up_weight, live_count, codes, dest, order):
+    slots, width = features.shape
+    taps = codes.shape[0]
+    deep, wide = down_weight.shape
+    rows = order.shape[1]
+    places = lax.axis_size("space")
+    cap = rows // places
+    bricks = rows // 8
+    wire = jnp.bfloat16
+    dma = pltpu.SemaphoreType.DMA
+    vmem = pl.BlockSpec(memory_space=pltpu.VMEM)
+    smem = pl.BlockSpec(memory_space=pltpu.SMEM)
+    return pl.pallas_call(
+        step_kernel,
+        out_shape=(
+            jax.ShapeDtypeStruct((slots, width), wire),
+            jax.ShapeDtypeStruct((8 * deep, width), jnp.float32),
+        ),
+        in_specs=[vmem, vmem, vmem, vmem, vmem, smem, vmem, vmem, vmem],
+        out_specs=(vmem, vmem),
+        scratch_shapes=[
+            pltpu.VMEM((slots, width), wire),
+            pltpu.VMEM((slots, width), wire),
+            pltpu.VMEM((width, slots + 256), wire),
+            pltpu.VMEM((width, (taps + 1) * width), wire),
+            pltpu.VMEM(((taps + 1) * width, slots), wire),
+            pltpu.VMEM((slots, width), jnp.float32),
+            pltpu.VMEM((slots, width), wire),
+            pltpu.VMEM((256, width), wire),
+            pltpu.VMEM((1, slots), jnp.float32),
+            pltpu.VMEM((slots, 128), jnp.float32),
+            pltpu.VMEM((rows, 128), jnp.float32),
+            pltpu.VMEM((places, cap, width), wire),
+            pltpu.VMEM((places, cap, width), wire),
+            pltpu.VMEM((places, cap, width), wire),
+            pltpu.VMEM((places, cap, width), wire),
+            pltpu.VMEM((places, cap, 2 * width), wire),
+            pltpu.VMEM((places, cap, 2 * width), wire),
+            pltpu.VMEM((rows, 2 * width), wire),
+            pltpu.VMEM((bricks, deep), wire),
+            pltpu.VMEM((bricks, deep), wire),
+            pltpu.VMEM((rows, 2 * width), wire),
+            pltpu.VMEM((slots, width), wire),
+            dma((2,)), dma((2,)), dma((places,)), dma((places,)), dma((places,)), dma((places,)),
+            dma((places,)), dma((places,)),
+        ],
+        compiler_params=pltpu.CompilerParams(collective_id=1, has_side_effects=True),
+        name="brick_step",
+    )(features, cotangent, conv_weight, down_weight, up_weight, live_count, codes, dest, order)
+
+
+def on_device(
+    features, cotangent, conv_weight, down_weight, up_weight, live_count, neighbours, destination, assemble
+):
+    slots, width = features.shape[1], features.shape[2]
+    deep, wide = down_weight.shape
+    taps = conv_weight.shape[0]
+    order = assemble[0, 0].reshape(-1, 8).T.reshape(1, -1)
+    output, block = whole_step(
+        features[0], cotangent[0], conv_weight, down_weight, up_weight, live_count,
+        neighbours[0], destination[0].reshape(1, slots), order,
     )
-
-
-def on_device(
-    features,
-    cotangent,
-    conv_weight,
-    down_weight,
-    up_weight,
-    live_count,
-    neighbours,
-    destination,
-    assemble,
-):
-    slots = features.shape[1]
-    width = features.shape[2]
-    places = lax.axis_size("space")
-    rim = slots // 8
-    cap = 2 * slots // places
-    zero_b = jnp.zeros((), jnp.bfloat16)
-    live = (jnp.arange(slots, dtype=jnp.int32) < live_count[0, 0])[:, None]
-    own = jnp.where(live, features[0], zero_b)
-    grad_rows = jnp.where(live, cotangent[0], zero_b)
-    dest = destination[0, :, 0]
-    onehot = (dest[:, None] == jnp.arange(places, dtype=jnp.int32)[None, :]).astype(jnp.int32)
-    rank = jnp.sum((jnp.cumsum(onehot, axis=0) - onehot) * onehot, axis=1)
-    target = dest * cap + rank
-
-    def pack(rows):
-        return (
-            jnp.zeros((2 * slots, width), rows.dtype)
-            .at[target]
-            .set(rows)
-            .reshape(places, cap, width)
-        )
-
-    codes = neighbours[0].T
-    zero_row = jnp.zeros((1, width), jnp.bfloat16)
-    padded = extended(own[None], (("space", 0),), 1)
-    table = jnp.concatenate([padded.reshape(3 * slots, width), zero_row], axis=0)
-    index = jnp.where(
-        codes < slots,
-        slots + codes,
-        jnp.where(codes < slots + rim, rim + codes - slots, 2 * slots + codes - slots - rim),
-    )
-    index = jnp.where(codes < 0, 3 * slots, index)
-    rows = table[index]
-    stacked = jnp.concatenate([own[:, None, :], rows], axis=1).reshape(slots, 27 * width)
-    pre_conv = jnp.dot(stacked, conv_weight, preferred_element_type=jnp.float32)
-    mixed = jnp.where(live, own.astype(jnp.float32) + jax.nn.silu(pre_conv), 0.0).astype(
-        jnp.bfloat16
-    )
-    stacked, pre_conv, mixed = (stacked, pre_conv, mixed)
-    got_mixed, got_grad = (
-        lax.all_to_all(pack(mixed), "space", split_axis=0, concat_axis=0, tiled=True),
-        lax.all_to_all(pack(grad_rows), "space", split_axis=0, concat_axis=0, tiled=True),
-    )
-    order = assemble[0, 0]
-    coarse_rows = 2 * slots // 8
-    coarse_in = got_mixed.reshape(2 * slots, width)[order].reshape(coarse_rows, 8 * width)
-    coarse_grad = got_grad.reshape(2 * slots, width)[order].reshape(coarse_rows, 8 * width)
-    pre = jnp.dot(coarse_in, down_weight, preferred_element_type=jnp.float32)
-    coarse = jax.nn.silu(pre).astype(jnp.bfloat16)
-    up_rows = jnp.dot(coarse, up_weight, preferred_element_type=jnp.float32).astype(jnp.bfloat16)
-    grad_up = contract_rows(coarse, coarse_grad)
-    back = contract_cols(coarse_grad, up_weight)
-    grad_pre = (back * silu_grad(pre)).astype(jnp.bfloat16)
-    grad_down = contract_rows(coarse_in, grad_pre)
-    grad_in = contract_cols(grad_pre, down_weight).astype(jnp.bfloat16)
-
-    def unpack(rows):
-        return (
-            jnp.zeros((2 * slots, width), jnp.bfloat16)
-            .at[order]
-            .set(rows.reshape(2 * slots, width))
-            .reshape(places, cap, width)
-        )
-
-    got_up, got_back = (
-        lax.all_to_all(unpack(up_rows), "space", split_axis=0, concat_axis=0, tiled=True),
-        lax.all_to_all(unpack(grad_in), "space", split_axis=0, concat_axis=0, tiled=True),
-    )
-    fine_up = got_up.reshape(2 * slots, width)[target]
-    fine_back = got_back.reshape(2 * slots, width)[target]
-    output = jnp.where(live, mixed.astype(jnp.float32) + fine_up.astype(jnp.float32), 0.0).astype(
-        jnp.bfloat16
-    )
-    grad_mixed = jnp.where(live, grad_rows.astype(jnp.float32) + fine_back.astype(jnp.float32), 0.0)
-    grad_conv_pre = (grad_mixed * silu_grad(pre_conv)).astype(jnp.bfloat16)
-    grad_conv = contract_rows(stacked, grad_conv_pre)
-    taps, wide = grad_conv.shape[0], grad_up.shape[0]
-    deep = grad_down.shape[0]
-    spare = jnp.zeros((deep * 4 - taps, width), jnp.float32)
-    down = grad_down.reshape(deep, wide // width, width).transpose(1, 0, 2).reshape(-1, width)
-    up = grad_up.reshape(wide, deep // width, width).transpose(1, 0, 2).reshape(-1, width)
-    block = jnp.concatenate([grad_conv, spare, down, up], axis=0)
     total = all_sum(block.reshape(2, 16, -1, width)).reshape(-1, width)
     grad_conv = total[:taps].astype(jnp.float32)
-    down = total[deep * 4 : deep * 4 + down.shape[0]].reshape(wide // width, deep, width)
-    up = total[deep * 4 + down.shape[0] * down.shape[1] :].reshape(deep // width, wide, width)
+    half = deep * wide // width
+    down = total[deep * 4 : deep * 4 + half].reshape(wide // width, deep, width)
+    up = total[deep * 4 + half :].reshape(deep // width, wide, width)
     grad_down = down.transpose(1, 0, 2).reshape(deep, wide).astype(jnp.float32)
     grad_up = up.transpose(1, 0, 2).reshape(wide, deep).astype(jnp.float32)
     return (output[None], grad_conv, grad_down, grad_up)

time: 258 us -> 149 us (0.58)
  local copies, waits for them, and re-layouts: 90.4 us -> 7.38 us
  Pallas kernels: 58.8 us -> 136 us
  starting transfers between devices: 40.6 us -> 0 us
  other arithmetic: 34 us -> 3.2 us
  waiting for transfers between devices: 16.1 us -> 0 us
  matrix products: 15.1 us -> 0 us
    pallas_call x0 -> x1, Pallas kernels: none -> 82.6 us  [whole_step(): pl.pallas_call(step_kernel, out_shape=(jax.ShapeDtypeStruct((slots, width...]
    gather x6 -> x0, local copies, waits for them, and re-layouts: 59.7 us -> none  [the longest x2 49.5 us: on_device(): rows = table[index]]
    all_to_all x4 -> x0, starting transfers between devices: 34.2 us -> none  [the longest x1 13 us: on_device(): lax.all_to_all(pack(grad_rows), 'space', split_axis=0, concat_axis=0, til...]
    concatenate x3 -> x0, other arithmetic: 17.9 us -> none  [the longest x1 8.98 us: on_device(): block = jnp.concatenate([grad_conv, spare, down, up], axis=0)]
    all_to_all x4 -> x0, waiting for transfers between devices: 16.1 us -> none  [the longest x1 10.3 us: on_device(): lax.all_to_all(pack(mixed), 'space', split_axis=0, concat_axis=0, tiled=T...]
    scatter x3 -> x0, local copies, waits for them, and re-layouts: 15.4 us -> none  [the longest x2 10.4 us: unpack(): return jnp.zeros((2 * slots, width), jnp.bfloat16).at[order].set(rows.res...]
    dot_general x8 -> x0, matrix products: 15.1 us -> none  [the longest x3 7 us: contract_rows(): lax.dot_general(left, right, (((0,), (0,)), ((), ())), preferred_element_...]
    concatenate x3 -> x0, local copies, waits for them, and re-layouts: 9.05 us -> none  [the longest x1 9 us: on_device(): jnp.concatenate([own[:, None, :], rows], axis=1).reshape(slots, 27 * width)]
  transfers between devices with their start and end apart: 6 -> 0, of which waited for: 2 -> 0; matrix products, arithmetic and copies ran while one was open for 49% -> 0% of each run, Pallas kernels for 23% -> 0%
where the time goes in v2:
time: 149 us; the launch traced here: 148 us
  Pallas kernels  136 us (91%)
  local copies, waits for them, and re-layouts  7.38 us (5%)
  other arithmetic  3.2 us (2%)
    pallas_call x1, Pallas kernels, whole_step(): pl.pallas_call(step_kernel, out_shape=(jax.ShapeDtypeStruct((slots, width...  82.6 us
    pallas_call x1, Pallas kernels, all_sum(): pl.pallas_call(reduce_kernel, out_shape=jax.ShapeDtypeStruct(block.shape,...  53.8 us
    unnamed x6, local copies, waits for them, and re-layouts  4.42 us

profile of v2, /device:TPU:1, one launch (start us, length us, event | category | flops | bytes accessed | tf_op | source)
XLA Modules:
  0.0 148.3 jit_solution(5383543114168183598)
XLA Ops:
  1.3 0.7 reduce
  2.0 0.1 reshape_squeeze.7
  2.1 0.1 copy.16
  2.2 0.7 reshape.29.order
  2.8 1.5 %copy.27 = s32[1,26,768]{2,1,0:T(8,128)} copy(s32[1,26,768]{2,0,1:T(1,128)} %param.15) | data formatting | bytes 159744
  4.4 82.6 %brick_step.1 = (bf16[768,128]{1,0:T(8,128)(2,1)}, f32[8192,128]{1,0:T(8,128)}) custom-call(bf16[768,128]{1,0:T(8,128)(2,1)} %bitcast.35, bf16[768,128]{1,0:T(8,128)(2,1)} %bitcast.36, bf16[3456,128]{1,0:T(8,128)(2,1)} %conv_weight.1, bf16[1024,256]{1,0:T(8,128)(2,1)} %down_weight.1, bf16[256,1024]{1,0:T(8,128)(2,1)} %up_weight.1, ...), custom_call_target="tpu_custom_call" | custom-call | tf_op jit(solution)/shard_map/brick_step/pallas_call | solution.py:514
  87.0 53.8 %sum_gradients.1 = bf16[2,16,256,128]{3,2,1,0:T(8,128)(2,1)} custom-call(f32[2,16,256,128]{3,2,1,0:T(8,128)} %bitcast.26), custom_call_target="tpu_custom_call" | custom-call | tf_op jit(solution)/shard_map/sum_gradients/pallas_call | solution.py:190
  140.8 1.3 fusion
  142.0 2.5 %slice_convert_fusion = f32[3456,128]{1,0:T(8,128)} fusion(bf16[8192,128]{1,0:T(8,128)(2,1)} %bitcast.25), kind=kLoop, calls=%fused_computation.2 | loop fusion | flops 442368 | bytes 2654208 | tf_op jit(solution)/shard_map/convert_element_type | solution.py:565
  144.5 0.5 copy.17
  145.1 1.0 copy.26
  146.1 0.0 copy-start
  146.1 0.3 copy.18
  146.4 1.2 copy.25
  147.6 0.0 copy-done
  147.6 0.7 copy.30
Async XLA Ops:
  146.1 1.5 copy-start

commit v3 on v2

--- a/solution.py
+++ b/solution.py
@@ -23,14 +23,17 @@
     return {"scene": y, "space": (z * 4 + x) * 2 + c}
 
 
-def reduce_kernel(
+def reducer(
     src, out, send_c, recv_c, send_p, recv_p, send_z, recv_z, acc, sem_cs, sem_cr, sem_ps, sem_pr,
     sem_zs, sem_zr, sem_gzs, sem_gzr, sem_gps, sem_gpr, sem_gcs, sem_gcr,
 ):
     y, z, x, c = place()
     q = x * 4 + y
-    part = src.shape[2]
+    part, width = acc.shape
     small = part // 8
+
+    def local(half, index):
+        return src[pl.ds(pl.multiple_of((half * 16 + index) * part, part), part), :]
 
     def plane(k):
         other = (q + k) % 16
@@ -44,20 +47,20 @@
         return pl.ds(pl.multiple_of(index * small, small), small)
 
     partner = peer(y, z, x, 1 - c)
-    barrier = pltpu.get_barrier_semaphore()
-    pl.semaphore_signal(barrier, inc=1, device_id=partner, device_id_type=MESH)
-
-    def greet_plane(k, carry):
-        pl.semaphore_signal(barrier, inc=1, device_id=plane(k)[1], device_id_type=MESH)
-        return carry
-
-    def greet_column(k, carry):
-        pl.semaphore_signal(barrier, inc=1, device_id=column(k)[1], device_id_type=MESH)
-        return carry
-
-    lax.fori_loop(1, 16, greet_plane, 0)
-    lax.fori_loop(1, 8, greet_column, 0)
-    pl.semaphore_wait(barrier, 23)
+
+    def greet(barrier):
+        pl.semaphore_signal(barrier, inc=1, device_id=partner, device_id_type=MESH)
+
+        def greet_plane(k, carry):
+            pl.semaphore_signal(barrier, inc=1, device_id=plane(k)[1], device_id_type=MESH)
+            return carry
+
+        def greet_column(k, carry):
+            pl.semaphore_signal(barrier, inc=1, device_id=column(k)[1], device_id_type=MESH)
+            return carry
+
+        lax.fori_loop(1, 16, greet_plane, 0)
+        lax.fori_loop(1, 8, greet_column, 0)
 
     def core_copy(k):
         return pltpu.make_async_remote_copy(
@@ -79,133 +82,124 @@
 
     def to_core(j, carry):
         k = (j + 1) % 16
-        send_c[k] = src[1 - c, plane(k)[0]].astype(jnp.bfloat16)
+        send_c[k] = local(1 - c, plane(k)[0]).astype(jnp.bfloat16)
         core_copy(k).start()
         return carry
-
-    lax.fori_loop(0, 16, to_core, 0)
 
     def to_plane(k, carry):
         core_copy(k).wait_recv()
-        total = src[c, plane(k)[0]] + recv_c[k].astype(jnp.float32)
+        total = local(c, plane(k)[0]) + recv_c[k].astype(jnp.float32)
         send_p[k] = total.astype(jnp.bfloat16)
         plane_copy(k).start()
         return carry
 
-    lax.fori_loop(1, 16, to_plane, 0)
-    core_copy(0).wait_recv()
-    acc[...] = src[c, q] + recv_c[0].astype(jnp.float32)
-
-    def add_plane(k, carry):
-        plane_copy(k).wait_recv()
-        acc[...] += recv_p[k].astype(jnp.float32)
-        return carry
-
-    lax.fori_loop(1, 16, add_plane, 0)
-
-    def to_column(k, carry):
-        send_z[k] = acc[rows(column(k)[0]), :].astype(jnp.bfloat16)
-        column_copy(k).start()
-        return carry
-
-    lax.fori_loop(1, 8, to_column, 0)
-
-    def add_column(k, total):
-        column_copy(k).wait_recv()
-        return total + recv_z[k].astype(jnp.float32)
-
-    total = lax.fori_loop(1, 8, add_column, acc[rows(z), :])
-    out[c, q, rows(z), :] = total.astype(jnp.bfloat16)
-
-    def gather_column(k, source):
-        piece = out.at[c, q, rows(source), :]
-        return pltpu.make_async_remote_copy(
-            src_ref=piece, dst_ref=piece, send_sem=sem_gzs.at[k], recv_sem=sem_gzr.at[k],
-            device_id=column(k)[1], device_id_type=MESH,
-        )
-
-    def gather_plane(k, source):
-        piece = out.at[c, source]
-        return pltpu.make_async_remote_copy(
-            src_ref=piece, dst_ref=piece, send_sem=sem_gps.at[k], recv_sem=sem_gpr.at[k],
-            device_id=plane(k)[1], device_id_type=MESH,
-        )
-
-    def gather_core(k, half):
-        piece = out.at[half, (q - k + 16) % 16]
-        return pltpu.make_async_remote_copy(
-            src_ref=piece, dst_ref=piece, send_sem=sem_gcs.at[k], recv_sem=sem_gcr.at[k],
-            device_id=partner, device_id_type=MESH,
-        )
-
-    def start_column(k, carry):
-        gather_column(k, z).start()
-        return carry
-
-    def wait_column(k, carry):
-        gather_column(k, (z - k + 8) % 8).wait_recv()
-        return carry
-
-    def start_plane(k, carry):
-        gather_plane(k, q).start()
-        return carry
-
-    def pass_core(k, carry):
-        gather_plane(k, (q - k + 16) % 16).wait_recv()
-        gather_core(k, c).start()
-        return carry
-
-    lax.fori_loop(1, 8, start_column, 0)
-    lax.fori_loop(1, 8, wait_column, 0)
-    lax.fori_loop(1, 16, start_plane, 0)
-    gather_core(0, c).start()
-    lax.fori_loop(1, 16, pass_core, 0)
-
-    def drain_core(k, carry):
-        gather_core(k, 1 - c).wait_recv()
-        gather_core(k, c).wait_send()
-        core_copy(k).wait_send()
-        return carry
-
-    def drain_plane(k, carry):
-        gather_plane(k, q).wait_send()
-        plane_copy(k).wait_send()
-        return carry
-
-    def drain_column(k, carry):
-        gather_column(k, z).wait_send()
-        column_copy(k).wait_send()
-        return carry
-
-    lax.fori_loop(0, 16, drain_core, 0)
-    lax.fori_loop(1, 16, drain_plane, 0)
-    lax.fori_loop(1, 8, drain_column, 0)
-
-
-def all_sum(block):
-    part = block.shape[2]
-    width = block.shape[3]
-    dma = pltpu.SemaphoreType.DMA
-    wire = jnp.bfloat16
-    return pl.pallas_call(
-        reduce_kernel,
-        out_shape=jax.ShapeDtypeStruct(block.shape, wire),
-        in_specs=[pl.BlockSpec(memory_space=pltpu.VMEM)],
-        out_specs=pl.BlockSpec(memory_space=pltpu.VMEM),
-        scratch_shapes=[
-            pltpu.VMEM((16, part, width), wire),
-            pltpu.VMEM((16, part, width), wire),
-            pltpu.VMEM((16, part, width), wire),
-            pltpu.VMEM((16, part, width), wire),
-            pltpu.VMEM((8, part // 8, width), wire),
-            pltpu.VMEM((8, part // 8, width), wire),
-            pltpu.VMEM((part, width), jnp.float32),
-            dma((16,)), dma((16,)), dma((16,)), dma((16,)), dma((8,)), dma((8,)),
-            dma((8,)), dma((8,)), dma((16,)), dma((16,)), dma((16,)), dma((16,)),
-        ],
-        compiler_params=pltpu.CompilerParams(collective_id=0, has_side_effects=True),
-        name="sum_gradients",
-    )(block)
+    def begin():
+        @pl.when(c == 0)
+        def _():
+            lax.fori_loop(0, 16, to_core, 0)
+
+        @pl.when(c == 1)
+        def _():
+            lax.fori_loop(1, 16, to_plane, 0)
+
+    def finish():
+        @pl.when(c == 1)
+        def _():
+            lax.fori_loop(0, 16, to_core, 0)
+
+        @pl.when(c == 0)
+        def _():
+            lax.fori_loop(1, 16, to_plane, 0)
+
+        core_copy(0).wait_recv()
+        acc[...] = local(c, q) + recv_c[0].astype(jnp.float32)
+
+        def add_plane(k, carry):
+            plane_copy(k).wait_recv()
+            acc[...] += recv_p[k].astype(jnp.float32)
+            return carry
+
+        lax.fori_loop(1, 16, add_plane, 0)
+
+        def to_column(k, carry):
+            send_z[k] = acc[rows(column(k)[0]), :].astype(jnp.bfloat16)
+            column_copy(k).start()
+            return carry
+
+        lax.fori_loop(1, 8, to_column, 0)
+
+        def add_column(k, total):
+            column_copy(k).wait_recv()
+            return total + recv_z[k].astype(jnp.float32)
+
+        total = lax.fori_loop(1, 8, add_column, acc[rows(z), :])
+        out[c, q, rows(z), :] = total.astype(jnp.bfloat16)
+
+        def gather_column(k, source):
+            piece = out.at[c, q, rows(source), :]
+            return pltpu.make_async_remote_copy(
+                src_ref=piece, dst_ref=piece, send_sem=sem_gzs.at[k], recv_sem=sem_gzr.at[k],
+                device_id=column(k)[1], device_id_type=MESH,
+            )
+
+        def gather_plane(k, source):
+            piece = out.at[c, source]
+            return pltpu.make_async_remote_copy(
+                src_ref=piece, dst_ref=piece, send_sem=sem_gps.at[k], recv_sem=sem_gpr.at[k],
+                device_id=plane(k)[1], device_id_type=MESH,
+            )
+
+        def gather_core(k, half):
+            piece = out.at[half, (q - k + 16) % 16]
+            return pltpu.make_async_remote_copy(
+                src_ref=piece, dst_ref=piece, send_sem=sem_gcs.at[k], recv_sem=sem_gcr.at[k],
+                device_id=partner, device_id_type=MESH,
+            )
+
+        def start_column(k, carry):
+            gather_column(k, z).start()
+            return carry
+
+        def wait_column(k, carry):
+            gather_column(k, (z - k + 8) % 8).wait_recv()
+            return carry
+
+        def start_plane(k, carry):
+            gather_plane(k, q).start()
+            return carry
+
+        def pass_core(k, carry):
+            gather_plane(k, (q - k + 16) % 16).wait_recv()
+            gather_core(k, c).start()
+            return carry
+
+        lax.fori_loop(1, 8, start_column, 0)
+        lax.fori_loop(1, 8, wait_column, 0)
+        lax.fori_loop(1, 16, start_plane, 0)
+        gather_core(0, c).start()
+        lax.fori_loop(1, 16, pass_core, 0)
+
+        def drain_core(k, carry):
+            gather_core(k, 1 - c).wait_recv()
+            gather_core(k, c).wait_send()
+            core_copy(k).wait_send()
+            return carry
+
+        def drain_plane(k, carry):
+            gather_plane(k, q).wait_send()
+            plane_copy(k).wait_send()
+            return carry
+
+        def drain_column(k, carry):
+            gather_column(k, z).wait_send()
+            column_copy(k).wait_send()
+            return carry
+
+        lax.fori_loop(0, 16, drain_core, 0)
+        lax.fori_loop(1, 16, drain_plane, 0)
+        lax.fori_loop(1, 8, drain_column, 0)
+
+    return greet, begin, finish
 
 
 def one_hot(condition):
@@ -224,10 +218,10 @@
 
 def step_kernel(
     features, cotangent, conv_weight, down_weight, up_weight, live_count, codes, dest, order,
-    output, block,
+    output, summed, block,
     own, grads, table, weight_t, stacked, pre_fine, mixed, rim, target_row, target_col, order_col,
     send_m, recv_m, send_g, recv_g, send_u, recv_u, joined, coarse_in, coarse_grad, returned, slope,
-    sem_rs, sem_rr, sem_ms, sem_mr, sem_gs, sem_gr, sem_us, sem_ur,
+    sem_rs, sem_rr, sem_ms, sem_mr, sem_gs, sem_gr, sem_us, sem_ur, *sum_scratch,
 ):
     y, z, x, c = place()
     me = (z * 4 + x) * 2 + c
@@ -238,6 +232,7 @@
     span = group * cap
     bricks = coarse_in.shape[0]
     taps = codes.shape[0]
+    sum_greet, sum_begin, sum_finish = reducer(block, summed, *sum_scratch)
 
     def at(device):
         return {"scene": y, "space": device}
@@ -252,6 +247,7 @@
         return carry
 
     lax.fori_loop(1, places, greet, 0)
+    sum_greet(barrier)
 
     count = live_count[0, 0]
     live = iota((slots, width), 0) < count
@@ -275,7 +271,7 @@
         cols = slice(part * 128, part * 128 + 128)
         order_col[cols, :] = jnp.broadcast_to(order[:, cols].astype(jnp.float32), (128, 128)).T
 
-    pl.semaphore_wait(barrier, places - 1)
+    pl.semaphore_wait(barrier, places - 1 + 23)
 
     def rim_copy(upward):
         start = edge if upward else 0
@@ -460,6 +456,8 @@
     for k in range(deep // width):
         block[base + k * wide : base + (k + 1) * wide, :] = grad_up[:, k * width : k * width + width]
 
+    sum_begin()
+
     arrived(recv_u, send_u, sem_us, sem_ur)
     flat(recv_u, 2 * width, 0)
 
@@ -485,6 +483,7 @@
 
     lax.fori_loop(0, 9, convolve, 0)
     block[27 * width : 4 * deep, :] = jnp.zeros((4 * deep - 27 * width, width), jnp.float32)
+    sum_finish()
 
     left(recv_g, send_g, sem_gs, sem_gr)
     left(recv_m, send_m, sem_ms, sem_mr)
@@ -515,11 +514,12 @@
         step_kernel,
         out_shape=(
             jax.ShapeDtypeStruct((slots, width), wire),
-            jax.ShapeDtypeStruct((8 * deep, width), jnp.float32),
+            jax.ShapeDtypeStruct((2, 16, deep // 4, width), wire),
         ),
         in_specs=[vmem, vmem, vmem, vmem, vmem, smem, vmem, vmem, vmem],
         out_specs=(vmem, vmem),
         scratch_shapes=[
+            pltpu.VMEM((8 * deep, width), jnp.float32),
             pltpu.VMEM((slots, width), wire),
             pltpu.VMEM((slots, width), wire),
             pltpu.VMEM((width, slots + 256), wire),
@@ -544,6 +544,15 @@
             pltpu.VMEM((slots, width), wire),
             dma((2,)), dma((2,)), dma((places,)), dma((places,)), dma((places,)), dma((places,)),
             dma((places,)), dma((places,)),
+            pltpu.VMEM((16, deep // 4, width), wire),
+            pltpu.VMEM((16, deep // 4, width), wire),
+            pltpu.VMEM((16, deep // 4, width), wire),
+            pltpu.VMEM((16, deep // 4, width), wire),
+            pltpu.VMEM((8, deep // 32, width), wire),
+            pltpu.VMEM((8, deep // 32, width), wire),
+            pltpu.VMEM((deep // 4, width), jnp.float32),
+            dma((16,)), dma((16,)), dma((16,)), dma((16,)), dma((8,)), dma((8,)),
+            dma((8,)), dma((8,)), dma((16,)), dma((16,)), dma((16,)), dma((16,)),
         ],
         compiler_params=pltpu.CompilerParams(collective_id=1, has_side_effects=True),
         name="brick_step",
@@ -557,11 +566,11 @@
     deep, wide = down_weight.shape
     taps = conv_weight.shape[0]
     order = assemble[0, 0].reshape(-1, 8).T.reshape(1, -1)
-    output, block = whole_step(
+    output, summed = whole_step(
         features[0], cotangent[0], conv_weight, down_weight, up_weight, live_count,
         neighbours[0], destination[0].reshape(1, slots), order,
     )
-    total = all_sum(block.reshape(2, 16, -1, width)).reshape(-1, width)
+    total = summed.reshape(-1, width)
     grad_conv = total[:taps].astype(jnp.float32)
     half = deep * wide // width
     down = total[deep * 4 : deep * 4 + half].reshape(wide // width, deep, width)

time: 149 us -> 131 us (0.88)
  Pallas kernels: 136 us -> 119 us
    pallas_call x1 -> x0, Pallas kernels: 53.8 us -> none  [all_sum(): pl.pallas_call(reduce_kernel, out_shape=jax.ShapeDtypeStruct(block.shape,...]
    pallas_call x1, Pallas kernels: 82.6 us -> 119 us  [whole_step(): pl.pallas_call(step_kernel, out_shape=(jax.ShapeDtypeStruct((slots, width...]
where the time goes in v3:
time: 131 us; the launch traced here: 130 us
  Pallas kernels  119 us (91%)
  local copies, waits for them, and re-layouts  7.38 us (6%)
  other arithmetic  3.2 us (2%)
  between operations  1.31 us (1%)
    pallas_call x1, Pallas kernels, whole_step(): pl.pallas_call(step_kernel, out_shape=(jax.ShapeDtypeStruct((slots, width...  119 us
    unnamed x6, local copies, waits for them, and re-layouts  4.42 us

profile of v3, /device:TPU:1, one launch (start us, length us, event | category | flops | bytes accessed | tf_op | source)
XLA Modules:
  0.0 130.4 jit_solution(3384745732408501685)
XLA Ops:
  1.3 0.7 reduce
  2.0 0.1 reshape_squeeze.7
  2.1 0.1 copy.16
  2.2 0.7 reshape.26.order
  2.8 1.5 %copy.27 = s32[1,26,768]{2,1,0:T(8,128)} copy(s32[1,26,768]{2,0,1:T(1,128)} %param.15) | data formatting | bytes 159744
  4.4 118.6 %brick_step.1 = (bf16[768,128]{1,0:T(8,128)(2,1)}, bf16[2,16,256,128]{3,2,1,0:T(8,128)(2,1)}) custom-call(bf16[768,128]{1,0:T(8,128)(2,1)} %bitcast.33, bf16[768,128]{1,0:T(8,128)(2,1)} %bitcast.34, bf16[3456,128]{1,0:T(8,128)(2,1)} %conv_weight.1, bf16[1024,256]{1,0:T(8,128)(2,1)} %down_weight.1, bf16[256,1024]{1,0:T(8,128)(2,1)} %up_weight.1, ...), custom_call_target="tpu_custom_call" | custom-call | tf_op jit(solution)/shard_map/brick_step/pallas_call | solution.py:513
  122.9 1.3 fusion
  124.2 2.5 %slice_convert_fusion = f32[3456,128]{1,0:T(8,128)} fusion(bf16[8192,128]{1,0:T(8,128)(2,1)} %bitcast.28), kind=kLoop, calls=%fused_computation.2 | loop fusion | flops 442368 | bytes 2654208 | tf_op jit(solution)/shard_map/convert_element_type | solution.py:574
  126.7 0.5 copy.17
  127.2 1.0 copy.26
  128.3 0.0 copy-start
  128.3 0.3 copy.18
  128.6 1.2 copy.25
  129.8 0.0 copy-done
  129.8 0.7 copy.30
Async XLA Ops:
  128.3 1.5 %copy-start = (bf16[768,128]{1,0:T(8,128)(2,1)S(1)}, bf16[768,128]{1,0:T(8,128)(2,1)}, u32[]{:S(2)}) copy-start(bf16[768,128]{1,0:T(8,128)(2,1)} %get-tuple-element.6) | copy-start | bytes 589828
